TPU v7x, 512 devices: a whole 4x8x8 slice. The times are simulated.
512 devices in a mesh: gx: 32 (over y, x), gy: 16 (over z, core).
Axes of the slice: x: 4, y: 8, z: 8, core: 2. Of those that a mesh axis runs over, the one named last changes fastest.
Arguments:
- rhs: float32 [8, 512, 2048], P(None, 'gx', 'gy'), may hold values from -6 to 6
- cond_class: int32 [8, 512, 2048], P(None, 'gx', 'gy'), may hold values from 0 to 15
- charge_class: int32 [8, 512, 2048], P(None, 'gx', 'gy'), may hold values from 0 to 15
- cond_table: float32 [16], replicated, may hold values from 0.1 to 1
- charge_table: float32 [16], replicated, may hold values from 0 to 0.5
Outputs:
- correction: float32 [8, 512, 2048], P(None, 'gx', 'gy')
- residual: float32 [8, 512, 2048], P(None, 'gx', 'gy')
All inputs are finite; a program needn't handle non-finite values.
Results may differ from a plain program's by a relative error of at most 0.0003.
Values sent between devices are 32-bit elements; how exact they have to be, the bound alone decides.
A program may use at most 64 MiB of HBM per device.

v0:
```python
import jax
import jax.numpy as jnp
from jax import lax
from jax.sharding import PartitionSpec as P

LEVELS = 4
PRE_SWEEPS = 2
POST_SWEEPS = 2
COARSE_SWEEPS = 6
CYCLES = 2


relax_weight = 0.9
shift_weight = 0.1


def extended(cells, sides, width):
    for axis, dim in sides:
        count = lax.axis_size(axis)
        ends = count - 1
        head = lax.slice_in_dim(cells, 0, width, axis=dim)
        tail = lax.slice_in_dim(cells, cells.shape[dim] - width, cells.shape[dim], axis=dim)
        cells = jnp.concatenate(
            [
                lax.ppermute(tail, axis, [(i, (i + 1) % count) for i in range(ends)]),
                cells,
                lax.ppermute(head, axis, [((i + 1) % count, i) for i in range(ends)]),
            ],
            axis=dim,
        )
    return cells


def blur_along(padded, along):
    extent = padded.shape[along] - 2
    lower_side = lax.slice_in_dim(padded, 0, extent, axis=along)
    middle = lax.slice_in_dim(padded, 1, extent + 1, axis=along)
    upper_side = lax.slice_in_dim(padded, 2, extent + 2, axis=along)
    return 0.5 * lower_side + middle + 0.5 * upper_side


def blur_cells(padded):
    along_y = blur_along(padded, 3)
    along_x = blur_along(along_y, 2)
    deeper = jnp.pad(along_x, ((0, 0), (1, 1), (0, 0), (0, 0)))
    return blur_along(deeper, 1)


def grid_rims(stacked):
    return extended(stacked, (("gx", 2), ("gy", 3)), 1)


def look_up(classes, table):
    looked_up = jnp.zeros(classes.shape, jnp.float32)
    for class_id in range(table.shape[0]):
        looked_up = jnp.where(classes == class_id, table[class_id], looked_up)
    return looked_up


def coarsen(field):
    depth_cells, width_x, width_y = field.shape
    blocks = field.reshape(depth_cells // 2, 2, width_x // 2, 2, width_y // 2, 2)
    return jnp.mean(blocks, axis=(1, 3, 5))


def refine(field):
    depth_cells, width_x, width_y = field.shape
    copies = jnp.broadcast_to(
        field[:, None, :, None, :, None], (depth_cells, 2, width_x, 2, width_y, 2)
    )
    return copies.reshape(2 * depth_cells, 2 * width_x, 2 * width_y)


def diagonal_of(conduct, factor, padder):
    blurred = blur_cells(padder(conduct[None]))[0]
    beside_all = 2.0 * blurred - 2.0 * conduct
    return factor * 0.5 * (14.0 * conduct + beside_all) + shift_weight * conduct


def operate(iterate, conduct, diagonal, factor, padder):
    flux_term = conduct * iterate
    blurred = blur_cells(padder(jnp.stack([iterate, flux_term])))
    near_iterate = 2.0 * blurred[0] - 2.0 * iterate
    near_flux = 2.0 * blurred[1] - 2.0 * flux_term
    return diagonal * iterate - factor * 0.5 * (conduct * near_iterate + near_flux)


def smooth(iterate, source, conduct, diagonal, factor, padder, sweeps):
    for repeat in range(sweeps):
        iterate = (
            iterate
            + relax_weight
            * (source - operate(iterate, conduct, diagonal, factor, padder))
            / diagonal
        )
    return iterate


def smooth_from_zero(source, conduct, diagonal, factor, padder, sweeps):
    iterate = relax_weight * source / diagonal
    return smooth(iterate, source, conduct, diagonal, factor, padder, sweeps - 1)


def per_device(rhs, cond_class, charge_class, cond_table, charge_table):
    conduct = look_up(cond_class, cond_table) * (1.0 - look_up(charge_class, charge_table))
    conducts = [conduct]
    for grid_level in range(1, LEVELS):
        conducts.append(coarsen(conducts[-1]))
    factors = [0.25**grid_level for grid_level in range(LEVELS)]
    diagonals = [
        diagonal_of(conducts[grid_level], factors[grid_level], grid_rims)
        for grid_level in range(LEVELS - 1)
    ]
    last_level = LEVELS - 1
    coarse_tile = conducts[last_level]
    coarse_diagonal = diagonal_of(coarse_tile, factors[last_level], grid_rims)

    def coarse_solve(source):
        factor = factors[last_level]
        return smooth_from_zero(
            source, coarse_tile, coarse_diagonal, factor, grid_rims, COARSE_SWEEPS
        )

    def vcycle(grid_level, source):
        if grid_level == last_level:
            return coarse_solve(source)
        here_conduct = conducts[grid_level]
        here_diagonal = diagonals[grid_level]
        factor = factors[grid_level]
        iterate = smooth_from_zero(
            source, here_conduct, here_diagonal, factor, grid_rims, PRE_SWEEPS
        )
        remainder = source - operate(iterate, here_conduct, here_diagonal, factor, grid_rims)
        iterate = iterate + refine(vcycle(grid_level + 1, coarsen(remainder)))
        return smooth(iterate, source, here_conduct, here_diagonal, factor, grid_rims, POST_SWEEPS)

    correction = jnp.zeros_like(rhs)
    residual = rhs
    for repeat in range(CYCLES):
        correction = correction + vcycle(0, residual)
        residual = rhs - operate(correction, conducts[0], diagonals[0], factors[0], grid_rims)
    return (correction, residual)


def solution(mesh):
    placed = (P(None, "gx", "gy"), P(None, "gx", "gy"), P(None, "gx", "gy"), P(), P())
    return jax.shard_map(
        per_device,
        mesh=mesh,
        in_specs=placed,
        out_specs=(P(None, "gx", "gy"), P(None, "gx", "gy")),
        check_vma=False,
    )
```

profile of v0, /device:TPU:223, one launch (start us, length us, event | category | flops | bytes accessed | tf_op | source)
XLA Modules:
  0.0 857.3 jit_solution(13521676267965880986)
XLA Ops:
  4.6 21.1 %subtract_multiply_fusion = f32[8,16,128]{2,1,0:T(8,128)S(1)} fusion(s32[8,16,128]{2,1,0:T(8,128)} %param.7, s32[8,16,128]{2,1,0:T(8,128)} %param.6, f32[]{:T(128)} %bitcast.31, f32[]{:T(128)} %bitcast.30, f32[]{:T(128)} %bitcast.29, f32[]{:T(128)} %bitcast.28, f32[]{:T(128)} %bitcast.27, f32[]{:T(128)} %bitcast.26, f32[]{:T(128)} %bitcast.25, f32[]{:T(128)} %bitcast.24, ...), kind=kLoop, calls=%fused_computation.491 | loop fusion | flops 1081344 | bytes 196736 | tf_op jit(solution)/shard_map/mul | solution.py:105
  25.6 4.3 collective-permute-start
  31.9 5.5 reshape.1616
  40.1 6.7 collective-permute-start.12
  57.5 7.4 collective-permute-start.2
  66.9 4.8 collective-permute-start.26
  74.0 6.7 collective-permute-start.4
  82.8 5.7 collective-permute-done.5
  88.7 6.3 collective-permute-start.6
  97.0 4.8 collective-permute-start.14
  114.0 6.0 collective-permute-start.10
  122.6 5.6 collective-permute-done.11
  128.6 5.5 reshape.1615
  151.4 4.8 collective-permute-done.19
  183.2 4.9 collective-permute-done.29
  193.6 4.3 collective-permute-done.31
  203.5 4.3 collective-permute-done.33
  212.8 4.3 collective-permute-done.35
  242.0 4.3 collective-permute-done.41
  261.1 4.3 collective-permute-done.45
  280.1 4.3 collective-permute-done.49
  318.1 4.3 collective-permute-done.57
  337.4 4.3 collective-permute-done.61
  346.8 4.3 collective-permute-done.63
  356.6 4.3 collective-permute-done.65
  366.0 4.3 collective-permute-done.67
  376.2 4.3 collective-permute-done.69
  385.6 4.9 collective-permute-done.71
  396.1 4.3 collective-permute-done.73
  405.7 4.6 collective-permute-done.75
  422.5 4.3 collective-permute-done.77
  432.6 5.6 collective-permute-done.79
  443.9 4.3 collective-permute-done.81
  453.9 5.6 collective-permute-done.83
  465.3 4.3 collective-permute-done.85
  475.3 5.6 collective-permute-done.87
  486.7 4.3 collective-permute-done.89
  496.6 5.6 collective-permute-done.91
  508.0 4.3 collective-permute-done.93
  518.0 5.6 collective-permute-done.95
  524.0 5.5 reshape.1620
  537.5 4.3 collective-permute-done.97
  546.7 4.9 collective-permute-done.99
  578.6 4.3 collective-permute-done.105
  588.0 4.3 collective-permute-done.107
  597.8 4.3 collective-permute-done.109
  607.2 4.3 collective-permute-done.111
  617.2 4.3 collective-permute-done.113
  655.2 4.3 collective-permute-done.121
  693.3 4.3 collective-permute-done.129
  712.5 4.3 collective-permute-done.133
  721.9 4.3 collective-permute-done.135
  731.7 4.3 collective-permute-done.137
  741.1 4.3 collective-permute-done.139
  751.3 4.3 collective-permute-done.141
  760.8 4.9 collective-permute-done.143
  771.2 4.3 collective-permute-done.145
  781.0 4.4 collective-permute-done.147
  797.6 4.3 collective-permute-done.149
  807.7 5.6 collective-permute-done.151
  819.0 4.3 collective-permute-done.153
  829.0 5.6 collective-permute-done.155
  840.4 4.3 collective-permute-done.157
  850.4 5.6 collective-permute-done.159
  (609 shorter events, 528.0 us)
Async XLA Ops:
  25.6 31.7 %collective-permute-start = (f32[1,8,1,128]{3,2,1,0:T(1,128)S(1)}, f32[1,8,1,128]{3,2,1,0:T(1,128)S(1)}, u32[]{:S(2)}, u32[]{:S(2)}) collective-permute-start(f32[1,8,1,128]{3,2,1,0:T(1,128)S(1)} %get-tuple-element.139), channel_id=1, source_target_pairs={{0,16},{16,32},{32,48},{48,64},{64,80},{80,96},{96,112},{112,128},... | collective-permute-start | bytes 12296 | tf_op jit(solution)/shard_map/ppermute | solution.py:25
  30.0 27.4 %collective-permute-start.1 = (f32[1,8,1,128]{3,2,1,0:T(1,128)S(1)}, f32[1,8,1,128]{3,2,1,0:T(1,128)S(1)}, u32[]{:S(2)}, u32[]{:S(2)}) collective-permute-start(f32[1,8,1,128]{3,2,1,0:T(1,128)S(1)} %get-tuple-element.140), channel_id=1, source_target_pairs={{16,0},{32,16},{48,32},{64,48},{80,64},{96,80},{112,96},{128,112},... | collective-permute-start | bytes 12296 | tf_op jit(solution)/shard_map/ppermute | solution.py:27
  40.1 40.7 %collective-permute-start.12 = (f32[1,4,1,64]{3,2,1,0:T(1,128)S(1)}, f32[1,4,1,64]{3,2,1,0:T(1,128)S(1)}, u32[]{:S(2)}, u32[]{:S(2)}) collective-permute-start(f32[1,4,1,64]{3,2,1,0:T(1,128)S(1)} %get-tuple-element.192), channel_id=1, source_target_pairs={{0,16},{16,32},{32,48},{48,64},{64,80},{80,96},{96,112},{112,128},... | collective-permute-start | bytes 3080 | tf_op jit(solution)/shard_map/ppermute | solution.py:25
  47.4 8.0 collective-permute-start.24
  49.4 8.0 collective-permute-start.25
  55.4 27.3 %collective-permute-start.13 = (f32[1,4,1,64]{3,2,1,0:T(1,128)S(1)}, f32[1,4,1,64]{3,2,1,0:T(1,128)S(1)}, u32[]{:S(2)}, u32[]{:S(2)}) collective-permute-start(f32[1,4,1,64]{3,2,1,0:T(1,128)S(1)} %get-tuple-element.193), channel_id=1, source_target_pairs={{16,0},{32,16},{48,32},{64,48},{80,64},{96,80},{112,96},{128,112},... | collective-permute-start | bytes 3080 | tf_op jit(solution)/shard_map/ppermute | solution.py:27
  57.5 14.3 %collective-permute-start.2 = (f32[1,8,18,1]{3,2,1,0:T(8,128)S(1)}, f32[1,8,18,1]{3,2,1,0:T(8,128)S(1)}, u32[]{:S(2)}, u32[]{:S(2)}) collective-permute-start(f32[1,8,18,1]{3,2,1,0:T(8,128)S(1)} %get-tuple-element.121), channel_id=1, source_target_pairs={{0,1},{1,2},{2,3},{3,4},{4,5},{5,6},{6,7},{7,8},{8,9},{9,10},{10,1... | collective-permute-start | bytes 1736 | tf_op jit(solution)/shard_map/ppermute | solution.py:25
  64.9 8.8 %collective-permute-start.3 = (f32[1,8,18,1]{3,2,1,0:T(8,128)S(1)}, f32[1,8,18,1]{3,2,1,0:T(8,128)S(1)}, u32[]{:S(2)}, u32[]{:S(2)}) collective-permute-start(f32[1,8,18,1]{3,2,1,0:T(8,128)S(1)} %get-tuple-element.122), channel_id=1, source_target_pairs={{1,0},{2,1},{3,2},{4,3},{5,4},{6,5},{7,6},{8,7},{9,8},{10,9},{11,1... | collective-permute-start | bytes 1736 | tf_op jit(solution)/shard_map/ppermute | solution.py:27
  66.9 75.2 %collective-permute-start.26 = (f32[1,2,6,1]{3,2,1,0:T(8,128)S(1)}, f32[1,2,6,1]{3,2,1,0:T(8,128)S(1)}, u32[]{:S(2)}, u32[]{:S(2)}) collective-permute-start(f32[1,2,6,1]{3,2,1,0:T(8,128)S(1)} %get-tuple-element.212), channel_id=1, source_target_pairs={{0,1},{1,2},{2,3},{3,4},{4,5},{5,6},{6,7},{7,8},{8,9},{9,10},{10,1... | collective-permute-start | bytes 152 | tf_op jit(solution)/shard_map/ppermute | solution.py:25
  71.8 70.3 %collective-permute-start.27 = (f32[1,2,6,1]{3,2,1,0:T(8,128)S(1)}, f32[1,2,6,1]{3,2,1,0:T(8,128)S(1)}, u32[]{:S(2)}, u32[]{:S(2)}) collective-permute-start(f32[1,2,6,1]{3,2,1,0:T(8,128)S(1)} %get-tuple-element.213), channel_id=1, source_target_pairs={{1,0},{2,1},{3,2},{4,3},{5,4},{6,5},{7,6},{8,7},{9,8},{10,9},{11,1... | collective-permute-start | bytes 152 | tf_op jit(solution)/shard_map/ppermute | solution.py:27
  74.0 8.7 %collective-permute-start.4 = (f32[2,8,1,128]{3,2,1,0:T(1,128)S(1)}, f32[2,8,1,128]{3,2,1,0:T(1,128)S(1)}, u32[]{:S(2)}, u32[]{:S(2)}) collective-permute-start(f32[2,8,1,128]{3,2,1,0:T(1,128)S(1)} %get-tuple-element.119), channel_id=1, source_target_pairs={{0,16},{16,32},{32,48},{48,64},{64,80},{80,96},{96,112},{112,128},... | collective-permute-start | bytes 24584 | tf_op jit(solution)/shard_map/ppermute | solution.py:25
  80.8 7.7 collective-permute-start.5
  88.7 13.1 %collective-permute-start.6 = (f32[2,8,18,1]{3,2,1,0:T(8,128)S(1)}, f32[2,8,18,1]{3,2,1,0:T(8,128)S(1)}, u32[]{:S(2)}, u32[]{:S(2)}) collective-permute-start(f32[2,8,18,1]{3,2,1,0:T(8,128)S(1)} %get-tuple-element.99), channel_id=1, source_target_pairs={{0,1},{1,2},{2,3},{3,4},{4,5},{5,6},{6,7},{7,8},{8,9},{9,10},{10,1... | collective-permute-start | bytes 3464 | tf_op jit(solution)/shard_map/ppermute | solution.py:25
  95.0 8.8 %collective-permute-start.7 = (f32[2,8,18,1]{3,2,1,0:T(8,128)S(1)}, f32[2,8,18,1]{3,2,1,0:T(8,128)S(1)}, u32[]{:S(2)}, u32[]{:S(2)}) collective-permute-start(f32[2,8,18,1]{3,2,1,0:T(8,128)S(1)} %get-tuple-element.100), channel_id=1, source_target_pairs={{1,0},{2,1},{3,2},{4,3},{5,4},{6,5},{7,6},{8,7},{9,8},{10,9},{11,1... | collective-permute-start | bytes 3464 | tf_op jit(solution)/shard_map/ppermute | solution.py:27
  97.0 9.2 %collective-permute-start.14 = (f32[1,4,10,1]{3,2,1,0:T(8,128)S(1)}, f32[1,4,10,1]{3,2,1,0:T(8,128)S(1)}, u32[]{:S(2)}, u32[]{:S(2)}) collective-permute-start(f32[1,4,10,1]{3,2,1,0:T(8,128)S(1)} %get-tuple-element.165), channel_id=1, source_target_pairs={{0,1},{1,2},{2,3},{3,4},{4,5},{5,6},{6,7},{7,8},{8,9},{9,10},{10,1... | collective-permute-start | bytes 488 | tf_op jit(solution)/shard_map/ppermute | solution.py:25
  101.8 7.7 collective-permute-start.15
  106.2 7.7 collective-permute-start.9
  114.0 8.6 %collective-permute-start.10 = (f32[2,8,18,1]{3,2,1,0:T(8,128)S(1)}, f32[2,8,18,1]{3,2,1,0:T(8,128)S(1)}, u32[]{:S(2)}, u32[]{:S(2)}) collective-permute-start(f32[2,8,18,1]{3,2,1,0:T(8,128)S(1)} %get-tuple-element.97), channel_id=1, source_target_pairs={{0,1},{1,2},{2,3},{3,4},{4,5},{5,6},{6,7},{7,8},{8,9},{9,10},{10,1... | collective-permute-start | bytes 3464 | tf_op jit(solution)/shard_map/ppermute | solution.py:25
  120.0 8.2 collective-permute-start.11
  138.7 7.7 collective-permute-start.17
  156.4 7.7 collective-permute-start.20
  158.4 7.7 collective-permute-start.21
  166.1 7.0 collective-permute-start.22
  180.5 7.6 collective-permute-start.29
  200.1 7.6 collective-permute-start.33
  219.7 7.6 collective-permute-start.37
  238.7 7.6 collective-permute-start.41
  257.7 7.6 collective-permute-start.45
  276.7 7.6 collective-permute-start.49
  295.7 7.6 collective-permute-start.53
  314.8 7.6 collective-permute-start.57
  334.0 7.6 collective-permute-start.61
  353.2 7.6 collective-permute-start.65
  372.8 7.7 collective-permute-start.69
  392.7 7.7 collective-permute-start.73
  419.1 7.7 collective-permute-start.77
  430.0 8.2 collective-permute-start.79
  440.6 7.7 collective-permute-start.81
  451.3 8.2 collective-permute-start.83
  461.9 7.7 collective-permute-start.85
  472.7 8.2 collective-permute-start.87
  483.3 7.7 collective-permute-start.89
  494.1 8.2 collective-permute-start.91
  504.6 7.7 collective-permute-start.93
  515.4 8.2 collective-permute-start.95
  534.1 7.7 collective-permute-start.97
  553.7 7.7 collective-permute-start.101
  575.2 7.6 collective-permute-start.105
  594.4 7.6 collective-permute-start.109
  613.8 7.6 collective-permute-start.113
  632.8 7.6 collective-permute-start.117
  651.8 7.6 collective-permute-start.121
  670.8 7.6 collective-permute-start.125
  689.9 7.6 collective-permute-start.129
  709.1 7.6 collective-permute-start.133
  728.3 7.6 collective-permute-start.137
  748.0 7.7 collective-permute-start.141
  767.8 7.7 collective-permute-start.145
  794.2 7.7 collective-permute-start.149
  805.1 8.2 collective-permute-start.151
  815.7 7.7 collective-permute-start.153
  826.4 8.2 collective-permute-start.155
  837.0 7.7 collective-permute-start.157
  847.8 8.2 collective-permute-start.159
  (98 other events, 592.3 us)
where the time goes:
time: 870 us; the launch traced here: 857 us
  starting transfers between devices  432 us (50%)
  waiting for transfers between devices  328 us (38%)
  local copies, waits for them, and re-layouts  52.5 us (6%)
  other arithmetic  39.8 us (5%)
    ppermute x80, waiting for transfers between devices, extended(): lax.ppermute(head, axis, [((i + 1) % count, i) for i in range(ends)])  322 us
    ppermute x80, starting transfers between devices, extended(): lax.ppermute(tail, axis, [(i, (i + 1) % count) for i in range(ends)])  225 us
    ppermute x80, starting transfers between devices, extended(): lax.ppermute(head, axis, [((i + 1) % count, i) for i in range(ends)])  207 us
    mul x1, other arithmetic, per_device(): look_up(cond_class, cond_table)  21.1 us
  transfers between devices with their start and end apart: 160, of which 82 were waited for; matrix products, arithmetic and copies ran while one was open for 3% of the time, Pallas kernels for 0%

commit v1 on v0

v1 whole, which is shorter than its diff:
```python
import functools

import jax
import jax.numpy as jnp
from jax import lax
from jax.experimental import pallas as pl
from jax.experimental.pallas import tpu as pltpu
from jax.sharding import PartitionSpec as P

MESH = pl.DeviceIdType.MESH
CYCLES = 2
COARSE_SWEEPS = 6
RELAX = 0.9
SHIFT = 0.1
DEPTH, WIDE, LONG = 8, 16, 128
REACH = (-4, -3, -2, -1, 1, 2, 3, 4)
SIDES = ((1, 0), (-1, 0), (0, 1), (0, -1), (1, 1), (1, -1), (-1, 1), (-1, -1))

FINE, MID, SHORT, FAR = 0, 24, 48, 54
COPIES = 78


def roll(x, shift, axis):
    shift %= x.shape[axis]
    return pltpu.roll(x, shift, axis) if shift else x


def pick(x, index):
    return jnp.take_along_axis(x, index, axis=1)


def blur(fields):
    along = []
    for v in fields:
        y = v + 0.5 * (roll(v, 1, 1) + roll(v, -1, 1))
        along.append(y + 0.5 * (roll(y, 1, 0) + roll(y, -1, 0)))
    out = []
    for d, v in enumerate(along):
        beside = [along[e] for e in (d - 1, d + 1) if 0 <= e < len(along)]
        out.append(v + 0.5 * functools.reduce(jnp.add, beside) if beside else v)
    return out


def operate(v, c, big):
    spread = blur(v)
    flux = blur([a * b for a, b in zip(c, v)])
    return [g * a - (b * s + f) for g, a, b, s, f in zip(big, v, c, spread, flux)]


def sweep(v, f, c, w, big):
    return [a + q * (s - o) for a, q, s, o in zip(v, w, f, operate(v, c, big))]


def residual_of(v, f, c, big):
    return [s - o for s, o in zip(f, operate(v, c, big))]


def diagonal(c, level):
    shift = SHIFT * 4.0**level
    return [(6.0 + shift) * a + b for a, b in zip(c, blur(c))]


def weight(c, diag):
    return [jnp.where(a > 0.0, RELAX / jnp.where(a > 0.0, d, 1.0), 0.0) for a, d in zip(c, diag)]


def look_up(classes, table):
    bits = [(classes & (1 << b)) != 0 for b in range(4)]
    level = [table[i] for i in range(16)]
    for bit in bits:
        level = [jnp.where(bit, level[2 * i + 1], level[2 * i]) for i in range(len(level) // 2)]
    return level[0]


def kernel(gx_count, gy_count, rhs, cond, charge, cond_table, charge_table, out, res, *scratch):
    (C, W, D, F, VA, VB, K, PS, PR, T, C1, W1, D1, F1, X1, V1, R1, E1, G, S2, AS, AR, BS, BR, C2, W2, D2, F2, V2, G3, H2, H1,
     Z, send_sem, recv_sem) = scratch
    gx, gy = lax.axis_index("gx"), lax.axis_index("gy")

    def at(dx, dy):
        return (lax.rem(gx + (dx + gx_count), gx_count), lax.rem(gy + (dy + gy_count), gy_count))

    def copy(src, dst, number, where):
        return pltpu.make_async_remote_copy(
            src_ref=src, dst_ref=dst, send_sem=send_sem.at[number], recv_sem=recv_sem.at[number],
            device_id=where, device_id_type=MESH,
        )

    left_in, right_in = gy > 0, gy < gy_count - 1
    low_in = jnp.where(gx > 0, 1.0, 0.0)
    high_in = jnp.where(gx < gx_count - 1, 1.0, 0.0)
    lane = lax.broadcasted_iota(jnp.int32, (8, 128), 1)
    sub = lax.broadcasted_iota(jnp.int32, (8, 128), 0)
    lane24 = lax.broadcasted_iota(jnp.int32, (24, 128), 1)
    first, last = lane == 0, lane == 127
    above = jnp.where(sub == 0, 0.0, 0.5)
    below = jnp.where(sub == 7, 0.0, 0.5)
    yes_left = jnp.where(left_in, 1.0, 0.0)
    yes_right = jnp.where(right_in, 1.0, 0.0)


    def fine_copies(n, array, h):
        ends = (
            (array.at[0, pl.ds(24 - h, h)], array.at[0, pl.ds(8 - h, h)]),
            (array.at[0, pl.ds(8, h)], array.at[0, pl.ds(24, h)]),
            (PS.at[n], PR.at[n, 0, pl.ds(1, 2)]),
            (PS.at[n], PR.at[n, 1, pl.ds(1, 2)]),
            (PS.at[n, 1], PR.at[n, 0, 0]),
            (PS.at[n, 1], PR.at[n, 1, 0]),
            (PS.at[n, 0], PR.at[n, 0, 3]),
            (PS.at[n, 0], PR.at[n, 1, 3]),
        )
        return [copy(a, b, FINE + 8 * n + i, at(*SIDES[i])) for i, (a, b) in enumerate(ends)]

    def pack_edges(n, array):
        for b in range(2):
            packed = None
            for i in range(8):
                row = roll(array[0, 8 + 8 * b + i], 16 * i + 8, 1)
                packed = row if packed is None else jnp.where(lane >= 16 * i, row, packed)
            PS[n, b] = packed

    def unpack_edges(n, array, lo, hi):
        from_left = lax.rem(lane, 16) < 8
        for b in range(4):
            packed = jnp.where(from_left, PR[n, 0, b], PR[n, 1, b])
            for i in range(8):
                if lo <= 8 * b + i < hi:
                    array[1, 8 * b + i] = roll(packed, -(16 * i + 8), 1)

    def blur_row(t0, t1):
        a0, a1, b0, b1 = roll(t0, 1, 1), roll(t1, 1, 1), roll(t0, -1, 1), roll(t1, -1, 1)
        y0 = t0 + 0.5 * (jnp.where(first, a1, a0) + jnp.where(last, b1, b0))
        y1 = t1 + 0.5 * (jnp.where(first, a0, a1) + jnp.where(last, b0, b1))
        return [y + (above * roll(y, 1, 0) + below * roll(y, -1, 0)) for y in (y0, y1)]

    def blur_rows(row, lo, hi, use, flux=True):
        window = {}
        for r in range(lo - 1, hi + 1):
            v = row(r)
            fields = [v, [C[t, r] * v[t] for t in range(2)]] if flux else [v]
            window[r] = [blur_row(*f) for f in fields]
            q = r - 1
            if q >= lo:
                spread = [
                    [window[q][k][t] + 0.5 * (window[q - 1][k][t] + window[r][k][t]) for t in range(2)]
                    for k in range(len(fields))
                ]
                use(q, *spread)
                del window[q - 1]

    def fine_change(q, t, v, f, spread, flux):
        return f[t, q] - (D[t, q] * v - (C[t, q] * spread[t] + flux[t]))

    def fine_sweep(source, row, lo, hi, keep):
        def use(q, spread, flux):
            v = row(q)
            for t in range(2):
                keep(t, q, v[t] + W[t, q] * fine_change(q, t, v[t], source, spread, flux))

        blur_rows(row, lo, hi, use)

    def rows_of(array):
        return lambda r: [array[0, r], array[1, r]]

    def put(array):
        def keep(t, q, v):
            array[t, q] = v

        return keep

    def fine_pairs(t):
        return [T[t, pl.ds(2 * d, 24, stride=8), :] + T[t, pl.ds(2 * d + 1, 24, stride=8), :] for d in range(4)]

    twice = lax.rem(2 * lane24, 128)

    def along_pairs(v, index):
        return pick(v + roll(v, -1, 1), index)


    def mid_copies(n, source):
        return [copy(source, R1.at[n, i], MID + 8 * n + i, at(*SIDES[i])) for i in range(8)]

    def mid_whole(n, own):
        parts = []
        for middle, before, after in ((0, 4, 5), (None, 2, 3), (1, 6, 7)):
            rows = []
            for d in range(4):
                m = own[d] if middle is None else R1[n, middle, d]
                outer = jnp.where(lane < 32, R1[n, after, d], R1[n, before, d])
                rows.append(jnp.where(lane < 64, m, roll(outer, 64, 1)))
            parts.append(rows)
        return parts

    def pack2(a, b):
        return jnp.where(sub < 4, a, roll(b, 4, 0))

    spot = 2 * lax.rem(lane + 16, 32)

    def short_copies(n, count):
        k = n if n == 0 else n + 1
        src = AS.at[pl.ds(k, count)]
        return [copy(src, AR.at[s, pl.ds(k, count)], SHORT + 2 * n + s, at(0, (1, -1)[s])) for s in range(2)]

    def far_copies(n, count):
        k = n if n == 0 else n + 1
        src = BS.at[pl.ds(k, count)]
        return [
            copy(src, BR.at[4 - o, pl.ds(k, count)], FAR + 8 * n + i, at(o, 0)) for i, o in enumerate(REACH)
        ]

    def join_sides(k):
        left, right = AR[0, k], AR[1, k]
        return jnp.where(lane < 16, left, jnp.where(lane < 48, AS[k], right))

    def spread_far(k, array, mask):
        for g in range(5):
            pair = []
            for b in (2 * g, 2 * g + 1):
                block = BS[k] if b == 4 else jnp.zeros((8, 128), jnp.float32) if b == 9 else BR[b, k]
                if mask and b not in (4, 9):
                    there = jnp.where(jnp.logical_and(gx + (b - 4) >= 0, gx + (b - 4) < gx_count), 1.0, 0.0)
                    block = block * there
                pair.append(block)
            array[0, 8 * g : 8 * g + 8, :] = pack2(pair[0], pair[1])
            array[1, 8 * g : 8 * g + 8, :] = jnp.where(sub < 4, roll(pair[0], 4, 0), pair[1])

    def load(ref, count):
        return [ref[d] for d in range(count)]

    started = []

    def start(copies):
        for c in copies:
            c.start()
        started.extend(copies)
        return copies

    def arrive(copies):
        for c in copies:
            c.wait_recv()

    barrier = pltpu.get_barrier_semaphore()
    peers = list(SIDES) + [(o, 0) for o in REACH if abs(o) > 1]
    for peer in peers:
        pl.semaphore_signal(barrier, inc=1, device_id=at(*peer), device_id_type=MESH)

    for x in range(WIDE):
        where = pl.ds(x, DEPTH, stride=WIDE)
        F[0, 0, 8 + x] = rhs[where, :]
        C[0, 8 + x] = look_up(cond[where, :], cond_table) * (1.0 - look_up(charge[where, :], charge_table))
    pack_edges(0, C)
    pack_edges(1, F.at[0])
    T[...] = jnp.zeros_like(T)
    G[...] = jnp.zeros_like(G)
    G3[...] = jnp.zeros_like(G3)
    for q in range(8, 16):
        r = 2 * (q - 4)
        T[0, 8 * q : 8 * q + 8, :] = C[0, r] + C[0, r + 1]
    for d, v in enumerate(fine_pairs(0)):
        E1[d] = along_pairs(v, twice)[8:16] * (0.125 * 0.25)

    pl.semaphore_wait(barrier, len(peers))
    to_c = start(fine_copies(0, C, 7))
    to_f = start(fine_copies(1, F.at[0], 6))
    to_c1 = start(mid_copies(0, E1))

    arrive(to_c)
    unpack_edges(0, C, 1, 31)
    side = jnp.where(lane < 64, yes_right, yes_left)
    for r in range(1, 31):
        if r < 8 or r >= 24:
            mask = low_in if r < 8 else high_in
            C[0, r] = C[0, r] * mask
            C[1, r] = C[1, r] * (side * mask)
        else:
            C[1, r] = C[1, r] * side

    def coefficients(q, spread):
        for t in range(2):
            c = C[t, q]
            diag = (6.0 + SHIFT) * c + spread[t]
            inside = c > 0.0
            D[t, q] = diag + 2.0 * c
            W[t, q] = jnp.where(inside, RELAX / jnp.where(inside, diag, 1.0), 0.0)

    blur_rows(rows_of(C), 2, 30, coefficients, flux=False)

    for cycle in range(CYCLES):
        source = F.at[cycle]
        arrive(to_f)
        unpack_edges(1 + cycle, source, 2, 30)

        fine_sweep(source, lambda r: [W[t, r] * source[t, r] for t in range(2)], 3, 29, put(VB))
        held = {}

        def pair_up(q, spread, flux):
            v = [VB[0, q], VB[1, q]]
            for t in range(2):
                change = fine_change(q, t, v[t], source, spread, flux)
                if q % 2 == 0:
                    held[t] = change
                else:
                    at_row = 8 * (4 + q // 2)
                    T[t, at_row : at_row + 8, :] = held[t] + change

        blur_rows(rows_of(VB), 4, 28, pair_up)
        for d, (v0, v1) in enumerate(zip(fine_pairs(0), fine_pairs(1))):
            F1[cycle, d] = jnp.where(lane24 < 64, along_pairs(v0, twice), along_pairs(v1, twice)) * 0.125

        if cycle == 0:
            arrive(to_c1)
            whole = mid_whole(0, load(E1, 4))
            side = jnp.where(lane < 64, 1.0, jnp.where(lane < 96, yes_right, yes_left))
            for g, mask in enumerate((side * low_in, side, side * high_in)):
                for d in range(4):
                    C1[d, 8 * g : 8 * g + 8, :] = whole[g][d] * mask
            c1 = load(C1, 4)
            diag = diagonal(c1, 1)
            for d, w in enumerate(weight(c1, diag)):
                W1[d] = w
                D1[d] = diag[d] + 2.0 * c1[d]
            for d in range(2):
                G[d, 0:24, :] = c1[2 * d] + c1[2 * d + 1]
            c2 = []
            own = []
            for d in range(2):
                pairs = G[d, pl.ds(0, 16, stride=2), :] + G[d, pl.ds(1, 16, stride=2), :]
                c2.append(along_pairs(pairs, twice[:16]) * (0.125 * 0.25))
                pairs = G[d, pl.ds(8, 8, stride=2), :] + G[d, pl.ds(9, 8, stride=2), :]
                own.append(along_pairs(pairs, spot) * (0.125 * 0.25))
            AS[0] = pack2(own[0], own[1])
            own = []
            for d, v in enumerate(diagonal(c2, 2)):
                S2[d] = v
                own.append(pick(S2[d, 4:12, :], spot // 2))
            AS[1] = pack2(own[0], own[1])
            to_near_c = start(short_copies(0, 2))

        c1, w1, big1 = load(C1, 4), load(W1, 4), load(D1, 4)
        f1 = [F1[cycle, d] for d in range(4)]
        v1 = sweep([w * f for w, f in zip(w1, f1)], f1, c1, w1, big1)
        r1 = residual_of(v1, f1, c1, big1)
        own = []
        for d in range(2):
            G[d, 0:24, :] = r1[2 * d] + r1[2 * d + 1]
            pairs = G[d, pl.ds(8, 8, stride=2), :] + G[d, pl.ds(9, 8, stride=2), :]
            own.append(along_pairs(pairs, spot) * 0.125)
        k = 2 + cycle
        AS[k] = pack2(own[0], own[1])
        to_near = start(short_copies(1 + cycle, 1))
        to_f1 = start(mid_copies(1 + cycle, F1.at[cycle, :, pl.ds(8, 8), :]))

        if cycle == 0:
            arrive(to_near_c)
            side = jnp.where(lane < 16, yes_left, jnp.where(lane < 48, 1.0, yes_right))
            for j in range(2):
                BS[j] = join_sides(j) * side
            to_far_c = start(far_copies(0, 2))
        arrive(to_near)
        BS[k] = join_sides(k)
        to_far = start(far_copies(1 + cycle, 1))

        arrive(to_f1)
        whole = mid_whole(1 + cycle, [F1[cycle, d, 8:16, :] for d in range(4)])
        for g in range(3):
            for d in range(4):
                X1[d, 8 * g : 8 * g + 8, :] = whole[g][d]
        f1 = load(X1, 4)
        for d, v in enumerate(sweep([w * f for w, f in zip(w1, f1)], f1, c1, w1, big1)):
            V1[d] = v
        if cycle == 0:
            arrive(to_far_c)
            spread_far(0, C2, True)
            spread_far(1, D2, False)
            c2 = load(C2, 2)
            diag = load(D2, 2)
            for d, w in enumerate(weight(c2, diag)):
                W2[d] = w
                D2[d] = diag[d] + 2.0 * c2[d]
            G3[0:40, :] = c2[0] + c2[1]
            pairs = G3[pl.ds(0, 24, stride=2), :] + G3[pl.ds(1, 24, stride=2), :]
            c3 = [along_pairs(pairs, twice) * (0.125 * 0.25)]
            diag = diagonal(c3, 3)
            w3 = weight(c3, diag)
            big3 = [diag[0] + 2.0 * c3[0]]
            for j, v in enumerate((c3, w3, big3)):
                Z[j] = v[0]

        arrive(to_far)
        spread_far(k, F2, False)
        c2, w2, big2, f2 = load(C2, 2), load(W2, 2), load(D2, 2), load(F2, 2)
        v2 = sweep([w * f for w, f in zip(w2, f2)], f2, c2, w2, big2)
        for d in range(2):
            V2[d] = v2[d]
        r2 = residual_of(v2, f2, c2, big2)
        G3[0:40, :] = r2[0] + r2[1]

        pairs = G3[pl.ds(0, 24, stride=2), :] + G3[pl.ds(1, 24, stride=2), :]
        f3 = [along_pairs(pairs, twice) * 0.125]
        c3, w3, big3 = [Z[0]], [Z[1]], [Z[2]]
        v3 = [w3[0] * f3[0]]
        for _ in range(COARSE_SWEEPS - 1):
            v3 = sweep(v3, f3, c3, w3, big3)
        half = lane24 // 2
        up = pick(v3[0], half)
        H2[0, pl.ds(0, 24, stride=2), :] = up
        H2[0, pl.ds(1, 24, stride=2), :] = up

        c2, w2, big2, f2 = [[ref[d, 8:32, :] for d in range(2)] for ref in (C2, W2, D2, F2)]
        v2 = [V2[d, 8:32, :] + H2[0, 8:32, :] for d in range(2)]
        for _ in range(2):
            v2 = sweep(v2, f2, c2, w2, big2)
        down = jnp.where(lane24 < 96, 16 + half, half - 48)
        for d in range(2):
            up = pick(v2[d], down)
            H1[d, pl.ds(0, 24, stride=2), :] = up
            H1[d, pl.ds(1, 24, stride=2), :] = up

        c1, w1, big1, f1 = load(C1, 4), load(W1, 4), load(D1, 4), load(X1, 4)
        v1 = [V1[d] + H1[d // 2, 8:32, :] for d in range(4)]
        for _ in range(2):
            v1 = sweep(v1, f1, c1, w1, big1)
        for d in range(8):
            T[0, pl.ds(d, 24, stride=8), :] = v1[d // 2]

        near = lane // 2
        for q in range(6, 18):
            row = T[0, 8 * q : 8 * q + 8, :]
            up = [pick(row, near), pick(row, 64 + near)]
            for r in (2 * q - 8, 2 * q - 7):
                for t in range(2):
                    VA[t, r] = VB[t, r] + up[t]
        fine_sweep(source, rows_of(VA), 6, 26, put(VB))

        def add(t, q, v):
            K[t, q] = v if cycle == 0 else K[t, q] + v

        fine_sweep(source, rows_of(VB), 7, 25, add)

        def keep_residual(q, spread, flux):
            v = K[0, q]
            change = fine_change(q, 0, v, F.at[0], spread, flux)
            if cycle + 1 < CYCLES:
                F[cycle + 1, 0, q] = change
            else:
                res[pl.ds(q - 8, DEPTH, stride=WIDE), :] = change
                out[pl.ds(q - 8, DEPTH, stride=WIDE), :] = v

        blur_rows(rows_of(K), 8, 24, keep_residual)
        if cycle + 1 < CYCLES:
            pack_edges(2 + cycle, F.at[cycle + 1])
            to_f = start(fine_copies(2 + cycle, F.at[cycle + 1], 6))

    for c in started:
        c.wait_send()


def per_device(gx_count, gy_count, rhs, cond_class, charge_class, cond_table, charge_table):
    flat = (DEPTH * WIDE, LONG)
    f32 = jnp.float32
    tile = (8, 128)
    fine = pltpu.VMEM((2, 32) + tile, f32)
    mid = pltpu.VMEM((4, 24, 128), f32)
    low = pltpu.VMEM((2, 40, 128), f32)
    scratch = [
        fine, fine, fine, pltpu.VMEM((CYCLES, 2, 32) + tile, f32), fine, fine, fine,
        pltpu.VMEM((3, 2) + tile, f32), pltpu.VMEM((3, 2, 4) + tile, f32), pltpu.VMEM((2, 192, 128), f32),
        mid, mid, mid, pltpu.VMEM((CYCLES, 4, 24, 128), f32), mid, mid,
        pltpu.VMEM((3, 8, 4) + tile, f32), pltpu.VMEM((4,) + tile, f32),
        pltpu.VMEM((2, 32, 128), f32), pltpu.VMEM((2, 16, 128), f32),
        pltpu.VMEM((4,) + tile, f32), pltpu.VMEM((2, 4) + tile, f32),
        pltpu.VMEM((4,) + tile, f32), pltpu.VMEM((9, 4) + tile, f32),
        low, low, low, low, low, pltpu.VMEM((48, 128), f32),
        pltpu.VMEM((1, 48, 128), f32), pltpu.VMEM((2, 48, 128), f32), pltpu.VMEM((3, 24, 128), f32),
        pltpu.SemaphoreType.DMA((COPIES,)), pltpu.SemaphoreType.DMA((COPIES,)),
    ]
    vmem, smem = pl.BlockSpec(memory_space=pltpu.VMEM), pl.BlockSpec(memory_space=pltpu.SMEM)
    correction, residual = pl.pallas_call(
        functools.partial(kernel, gx_count, gy_count),
        out_shape=[jax.ShapeDtypeStruct(flat, f32)] * 2,
        in_specs=[vmem, vmem, vmem, smem, smem],
        out_specs=[vmem, vmem],
        scratch_shapes=scratch,
        compiler_params=pltpu.CompilerParams(collective_id=0, has_side_effects=True),
    )(rhs.reshape(flat), cond_class.reshape(flat), charge_class.reshape(flat), cond_table, charge_table)
    return correction.reshape(rhs.shape), residual.reshape(rhs.shape)


def solution(mesh):
    placed = (P(None, "gx", "gy"), P(None, "gx", "gy"), P(None, "gx", "gy"), P(), P())
    return jax.shard_map(
        functools.partial(per_device, mesh.shape["gx"], mesh.shape["gy"]),
        mesh=mesh,
        in_specs=placed,
        out_specs=(P(None, "gx", "gy"), P(None, "gx", "gy")),
        check_vma=False,
    )
```

time: 870 us -> 52 us (0.06)
  the two profiles are of different devices: /device:TPU:223 before, /device:TPU:2 now
where the time goes in v1:
time: 52 us; the launch traced here: 51.8 us
  Pallas kernels  49 us (94%)
  local copies, waits for them, and re-layouts  2.14 us (4%)
  between operations  0.65 us (1%)
    pallas_call x1, Pallas kernels, per_device(): pl.pallas_call(functools.partial(kernel, gx_count, gy_count), out_shape=[...  49 us
    unnamed x4, local copies, waits for them, and re-layouts  2.14 us

profile of v1, /device:TPU:2, one launch (start us, length us, event | category | flops | bytes accessed | tf_op | source)
XLA Modules:
  0.0 51.8 jit_solution(10472785363473153994)
XLA Ops:
  0.6 49.0 %shard_map.68 = (f32[128,128]{1,0:T(8,128)}, f32[128,128]{1,0:T(8,128)}) custom-call(f32[128,128]{1,0:T(8,128)} %bitcast.5, s32[128,128]{1,0:T(8,128)} %bitcast.6, s32[128,128]{1,0:T(8,128)} %bitcast.7, f32[16]{0:T(128)} %cond_table.1, f32[16]{0:T(128)} %charge_table.1), custom_call_target="tpu_custom_call" | custom-call | tf_op jit(solution)/shard_map/pallas_call | solution.py:479
  49.7 0.0 copy-start
  49.7 1.5 %copy.9 = f32[8,16,128]{2,1,0:T(8,128)} copy(f32[8,16,128]{2,1,0:T(8,128)} %bitcast.9) | data formatting | bytes 131072
  51.2 0.0 copy-done
  51.2 0.6 %copy.10 = f32[8,16,128]{2,1,0:T(8,128)} copy(f32[8,16,128]{2,1,0:T(8,128)S(1)} %bitcast.8) | data formatting | bytes 131072
Async XLA Ops:
  49.7 1.5 %copy-start = (f32[128,128]{1,0:T(8,128)S(1)}, f32[128,128]{1,0:T(8,128)}, u32[]{:S(2)}) copy-start(f32[128,128]{1,0:T(8,128)} %get-tuple-element.5) | copy-start | bytes 196612

commit v2 on v1

v2 whole, which is shorter than its diff:
```python
import functools

import jax
import jax.numpy as jnp
from jax import lax
from jax.experimental import pallas as pl
from jax.experimental.pallas import tpu as pltpu
from jax.sharding import PartitionSpec as P

MESH = pl.DeviceIdType.MESH
CYCLES = 2
COARSE_SWEEPS = 6
RELAX = 0.9
SHIFT = 0.1
DEPTH, WIDE, LONG = 8, 16, 128
OWN = 12
SIDES = ((1, 0), (-1, 0), (0, 1), (0, -1), (1, 1), (1, -1), (-1, 1), (-1, -1))
AROUND = tuple((a, b) for a in range(-5, 6) for b in (-1, 0, 1) if (a, b) != (0, 0))
NEARER = tuple(p for p in AROUND if abs(p[0]) < 5)

FINE, FINE_MORE, MID, FAR = 0, 16, 28, 31
COPIES = 34


def roll(x, shift, axis):
    shift %= x.shape[axis]
    return pltpu.roll(x, shift, axis) if shift else x


def pick(x, index):
    return jnp.take_along_axis(x, index, axis=1)


def blur(fields):
    along = []
    for v in fields:
        y = (v + v) + (roll(v, 1, 1) + roll(v, -1, 1))
        along.append((y + y) + (roll(y, 1, 0) + roll(y, -1, 0)))
    if len(along) == 1:
        return along
    pairs = [along[0]] + [a + b for a, b in zip(along, along[1:])] + [along[-1]]
    return [a + b for a, b in zip(pairs, pairs[1:])]


def operate(v, c, big):
    spread = blur(v)
    flux = blur([a * b for a, b in zip(c, v)])
    return [g * a - (b * s + f) for g, a, b, s, f in zip(big, v, c, spread, flux)]


def sweep(v, f, c, w, big):
    return [a + q * (s - o) for a, q, s, o in zip(v, w, f, operate(v, c, big))]


def residual_of(v, f, c, big):
    return [s - o for s, o in zip(f, operate(v, c, big))]


def diagonal(c, level, scale):
    own = scale * (6.0 + SHIFT * 4.0**level)
    return [own * a + b for a, b in zip(c, blur(c))]


def weight(c, diag):
    return [jnp.where(a > 0.0, RELAX / jnp.where(a > 0.0, d, 1.0), 0.0) for a, d in zip(c, diag)]


def look_up(classes, table):
    bits = [(classes & (1 << b)) != 0 for b in range(4)]
    level = [table[i] for i in range(16)]
    for bit in bits:
        level = [jnp.where(bit, level[2 * i + 1], level[2 * i]) for i in range(len(level) // 2)]
    return level[0]


def kernel(gx_count, gy_count, rhs_in, cond_in, charge_in, cond_table_in, charge_table_in, out, res, *scratch):
    (rhs, cond, charge, cond_table, charge_table, C, W, D, F, VA, VB, K, PS, PR, T, C1, W1, D1, F1, V1, E1, R1, E2, R2, G, S2,
     AS, BC, BF, BL, C2, W2, D2, F2, V2, G3, H2, H1, Z, send_sem, recv_sem, in_sem) = scratch
    gx, gy = lax.axis_index("gx"), lax.axis_index("gy")

    def at(dx, dy):
        return (lax.rem(gx + (dx + gx_count), gx_count), lax.rem(gy + (dy + gy_count), gy_count))

    def copy(src, dst, number, where):
        return pltpu.make_async_remote_copy(
            src_ref=src, dst_ref=dst, send_sem=send_sem.at[number], recv_sem=recv_sem.at[number],
            device_id=where, device_id_type=MESH,
        )

    barrier = pltpu.get_barrier_semaphore()
    for peer in AROUND:
        pl.semaphore_signal(barrier, inc=1, device_id=at(*peer), device_id_type=MESH)
    pairs = ((cond_table_in, cond_table), (charge_table_in, charge_table), (cond_in, cond), (charge_in, charge), (rhs_in, rhs))
    inputs = [pltpu.make_async_copy(a, b, in_sem.at[i]) for i, (a, b) in enumerate(pairs)]
    for c in inputs:
        c.start()

    left_in, right_in = gy > 0, gy < gy_count - 1
    low_in = jnp.where(gx > 0, 1.0, 0.0)
    high_in = jnp.where(gx < gx_count - 1, 1.0, 0.0)
    lane = lax.broadcasted_iota(jnp.int32, (8, 128), 1)
    sub = lax.broadcasted_iota(jnp.int32, (8, 128), 0)
    lane24 = lax.broadcasted_iota(jnp.int32, (24, 128), 1)
    first, last = lane == 0, lane == 127
    above = jnp.where(sub == 0, 0.0, 0.5)
    below = jnp.where(sub == 7, 0.0, 0.5)
    yes_left = jnp.where(left_in, 1.0, 0.0)
    yes_right = jnp.where(right_in, 1.0, 0.0)


    def fine_copies(n, array, h):
        ends = (
            (array.at[0, pl.ds(28 - h, h)], array.at[0, pl.ds(12 - h, h)]),
            (array.at[0, pl.ds(12, h)], array.at[0, pl.ds(28, h)]),
            (PS.at[n], PR.at[n, 0, pl.ds(3, 4)]),
            (PS.at[n], PR.at[n, 1, pl.ds(3, 4)]),
            (PS.at[n, pl.ds(2, 2)], PR.at[n, 0, pl.ds(1, 2)]),
            (PS.at[n, pl.ds(2, 2)], PR.at[n, 1, pl.ds(1, 2)]),
            (PS.at[n, pl.ds(0, 2)], PR.at[n, 0, pl.ds(7, 2)]),
            (PS.at[n, pl.ds(0, 2)], PR.at[n, 1, pl.ds(7, 2)]),
        )
        return [copy(a, b, FINE + 8 * n + i, at(*SIDES[i])) for i, (a, b) in enumerate(ends)]

    def more_copies(n, array, h):
        ends = (
            (array.at[0, pl.ds(24 - h, 4)], array.at[0, pl.ds(8 - h, 4)], 0),
            (array.at[0, pl.ds(12 + h, 4)], array.at[0, pl.ds(28 + h, 4)], 1),
            (PS.at[n, 1], PR.at[n, 0, 0], 4),
            (PS.at[n, 1], PR.at[n, 1, 0], 5),
            (PS.at[n, 2], PR.at[n, 0, 9], 6),
            (PS.at[n, 2], PR.at[n, 1, 9], 7),
        )
        return [copy(a, b, FINE_MORE + 6 * n + i, at(*SIDES[k])) for i, (a, b, k) in enumerate(ends)]

    def pack_edges(n, array):
        for b in range(4):
            packed = None
            for i in range(4):
                row = roll(array[0, OWN + 4 * b + i], 32 * i + 16, 1)
                packed = row if packed is None else jnp.where(lane >= 32 * i, row, packed)
            PS[n, b] = packed

    def unpack_edges(n, array, blocks, lo, hi):
        from_left = lax.rem(lane, 32) < 16
        for b in blocks:
            packed = jnp.where(from_left, PR[n, 0, b], PR[n, 1, b])
            for i in range(4):
                if lo <= 4 * b + i < hi:
                    array[1, 4 * b + i] = roll(packed, -(32 * i + 16), 1)

    def blur_row(t0, t1):
        b0, b1 = roll(t0, -1, 1), roll(t1, -1, 1)
        u0 = t0 + jnp.where(last, b1, b0)
        u1 = t1 + jnp.where(last, b0, b1)
        a0, a1 = roll(u0, 1, 1), roll(u1, 1, 1)
        y0 = u0 + jnp.where(first, a1, a0)
        y1 = u1 + jnp.where(first, a0, a1)
        return [y + (above * roll(y, 1, 0) + below * roll(y, -1, 0)) for y in (y0, y1)]

    def blur_rows(row, lo, hi, use, flux=True):
        before = pair = None
        for r in range(lo - 1, hi + 1):
            v = row(r)
            fields = [v, [C[t, r] * v[t] for t in range(2)]] if flux else [v]
            now = [blur_row(*f) for f in fields]
            if before is not None:
                two = [[a + b for a, b in zip(x, y)] for x, y in zip(before, now)]
                if pair is not None:
                    use(r - 1, *[[a + b for a, b in zip(x, y)] for x, y in zip(pair, two)])
                pair = two
            before = now

    def fine_change(q, t, v, f, spread, flux):
        return f[t, q] - (D[t, q] * v - (C[t, q] * spread[t] + flux[t]))

    def fine_sweep(source, row, lo, hi, keep):
        def use(q, spread, flux):
            v = row(q)
            for t in range(2):
                keep(t, q, v[t] + W[t, q] * fine_change(q, t, v[t], source, spread, flux))

        blur_rows(row, lo, hi, use)

    def rows_of(array):
        return lambda r: [array[0, r], array[1, r]]

    def put(array):
        def keep(t, q, v):
            array[t, q] = v

        return keep

    def mask_conductivity(rows):
        side = jnp.where(lane < 64, yes_right, yes_left)
        for r in rows:
            if OWN <= r < OWN + WIDE:
                C[1, r] = C[1, r] * side
            else:
                mask = low_in if r < OWN else high_in
                C[0, r] = C[0, r] * mask
                C[1, r] = C[1, r] * (side * mask)

    def coefficients(q, spread):
        for t in range(2):
            c = C[t, q]
            diag = (4.0 * (6.0 + SHIFT)) * c + spread[t]
            inside = c > 0.0
            D[t, q] = diag + 8.0 * c
            W[t, q] = jnp.where(inside, RELAX / jnp.where(inside, diag, 1.0), 0.0)

    def fine_pairs(t):
        return [T[t, pl.ds(2 * d, 24, stride=8), :] + T[t, pl.ds(2 * d + 1, 24, stride=8), :] for d in range(4)]

    twice = lax.rem(2 * lane24, 128)

    def along_pairs(v, index):
        return pick(v + roll(v, -1, 1), index)


    def two_in_one(a, b):
        return jnp.where(lane < 64, a, roll(b, 64, 1))

    def mid_copies(number, source, target):
        return [copy(source, target.at[i], number, at(*SIDES[i])) for i in range(8)]

    def mid_whole(own, arrived, keep):
        for g, (middle, before, after) in enumerate(((0, 4, 5), (None, 2, 3), (1, 6, 7))):
            for d in range(own.shape[0]):
                m = own[d] if middle is None else arrived[middle, d]
                outer = jnp.where(lane < 32, arrived[after, d], arrived[before, d])
                outer2 = jnp.where(lane < 96, arrived[after, d], arrived[before, d])
                keep(g, d, jnp.where(lane < 64, m, roll(outer, 64, 1)), jnp.where(lane < 64, roll(m, 64, 1), outer2))

    def stack_depth(a, b):
        return jnp.where(sub < 4, a, roll(b, 4, 0))


    spot = 2 * lax.rem(lane, 32)
    mid_side = jnp.where(lane < 64, 1.0, jnp.where(lane < 96, yes_right, yes_left))
    masks = (mid_side * low_in, mid_side, mid_side * high_in)

    def far_copies(n, target, peers):
        return [copy(AS.at[n], target.at[i], FAR + n, at(*p)) for i, p in enumerate(peers)]

    def far_block(n, arrived, peers, a, split):
        parts = []
        for b in (-1, 0, 1):
            parts.append(AS[n] if (a, b) == (0, 0) else arrived[peers.index((-a, -b))])
        if not split:
            return [jnp.where(lane < 32, parts[0], jnp.where(lane < 64, parts[1], parts[2]))]
        turned = [roll(p, 32, 1) for p in parts]
        return [
            jnp.where(lane < 32, parts[0], jnp.where(lane < 64, turned[1], parts[2])),
            jnp.where(lane < 32, turned[0], jnp.where(lane < 64, parts[1], turned[2])),
        ]

    def spread_far(n, arrived, peers, arrays, mask):
        split = len(arrays) == 2
        zero = jnp.zeros((8, 128), jnp.float32)
        reach = max(p[0] for p in peers)
        for g in range(6):
            pair = []
            for a in (2 * g - 5, 2 * g - 4):
                blocks = far_block(n, arrived, peers, a, split) if abs(a) <= reach else [zero] * len(arrays)
                if mask is not None and abs(a) <= reach:
                    there = jnp.where(jnp.logical_and(gx + a >= 0, gx + a < gx_count), 1.0, 0.0)
                    blocks[0] = blocks[0] * (mask * there)
                pair.append(blocks)
            for j, array in enumerate(arrays):
                array[0, 8 * g : 8 * g + 8, :] = stack_depth(pair[0][j], pair[1][j])
                array[1, 8 * g : 8 * g + 8, :] = jnp.where(sub < 4, roll(pair[0][j], 4, 0), pair[1][j])

    def load(ref, count):
        return [ref[d] for d in range(count)]

    ends = []

    def start(copies, group=None):
        for c in copies:
            c.start()
        if group is None:
            ends.extend(copies)
            return copies
        buffer, number = group
        whole = [copy(buffer, buffer, number, at(1, 0))]
        ends.extend(whole)
        return whole

    def arrive(copies):
        for c in copies:
            c.wait_recv()

    T[...] = jnp.zeros_like(T)
    G[...] = jnp.zeros_like(G)
    for c in inputs:
        c.wait()
    for x in range(WIDE):
        where = pl.ds(x, DEPTH, stride=WIDE)
        lost = 1.0 - look_up(charge[where, :], charge_table)
        C[0, OWN + x] = (look_up(cond[where, :], cond_table) * 0.25) * lost
        F[0, 0, OWN + x] = rhs[where, :]
    pack_edges(0, C)
    pack_edges(1, F.at[0])
    for q in range(8, 16):
        r = 2 * q - 4
        T[0, 8 * q : 8 * q + 8, :] = C[0, r] + C[0, r + 1]
    own = [along_pairs(v, twice)[8:16] * (0.125 * 0.125) for v in fine_pairs(0)]
    for d in range(2):
        E1[d] = two_in_one(own[d], own[d + 2])

    pl.semaphore_wait(barrier, len(AROUND))
    to_c = start(fine_copies(0, C, 7))
    to_f = start(fine_copies(1, F.at[0], 6))
    to_c1 = start(mid_copies(MID, E1, R1), (R1, MID))
    to_more = start(more_copies(0, C, 7)) + start(more_copies(1, F.at[0], 6))

    arrive(to_c)
    unpack_edges(0, C, range(1, 9), 5, 35)
    mask_conductivity(range(5, 35))
    blur_rows(rows_of(C), 6, 34, coefficients, flux=False)

    for cycle in range(CYCLES):
        source = F.at[cycle]
        final = cycle + 1 == CYCLES
        wide = 0 if final else 6

        if cycle == 0:
            arrive(to_f)
            unpack_edges(1, source, range(1, 9), 6, 34)

        def scaled(r):
            return [W[t, r] * source[t, r] for t in range(2)]

        fine_sweep(source, scaled, 7, 33, put(VB))
        held = {}

        def pair_up(q, spread, flux):
            v = [VB[0, q], VB[1, q]]
            for t in range(2):
                change = fine_change(q, t, v[t], source, spread, flux)
                if q % 2 == 0:
                    held[t] = change
                else:
                    at_row = 8 * (2 + q // 2)
                    T[t, at_row : at_row + 8, :] = held[t] + change

        blur_rows(rows_of(VB), 8, 32, pair_up)
        for d, (v0, v1) in enumerate(zip(fine_pairs(0), fine_pairs(1))):
            F1[d] = jnp.where(lane24 < 64, along_pairs(v0, twice), along_pairs(v1, twice)) * 0.125

        if cycle == 0:
            arrive(to_c1)

            def keep_c1(g, d, a, b):
                C1[d, 8 * g : 8 * g + 8, :] = a * masks[g]
                C1[d + 2, 8 * g : 8 * g + 8, :] = b * masks[g]

            mid_whole(E1, R1, keep_c1)
            c1 = load(C1, 4)
            diag = diagonal(c1, 1, 8.0)
            for d, w in enumerate(weight(c1, diag)):
                W1[d] = w
                D1[d] = diag[d] + 16.0 * c1[d]
            for d in range(2):
                G[d, 0:24, :] = c1[2 * d] + c1[2 * d + 1]
            c2 = []
            own = []
            for d in range(2):
                pairs = G[d, pl.ds(0, 16, stride=2), :] + G[d, pl.ds(1, 16, stride=2), :]
                c2.append(along_pairs(pairs, twice[:16]) * (0.125 * 0.25))
                pairs = G[d, pl.ds(8, 8, stride=2), :] + G[d, pl.ds(9, 8, stride=2), :]
                own.append(along_pairs(pairs, spot) * (0.125 * 0.25))
            own_d = []
            for d, v in enumerate(diagonal(c2, 2, 8.0)):
                S2[d] = v
                own_d.append(pick(S2[d, 4:12, :], spot // 2))
            AS[0] = jnp.where(lax.rem(lane, 64) < 32, stack_depth(*own), stack_depth(*own_d))
            to_far_c = start(far_copies(0, BC, AROUND), (BC, FAR))

        c1, w1, big1 = load(C1, 4), load(W1, 4), load(D1, 4)
        f1 = load(F1, 4)
        v1 = sweep([w * f for w, f in zip(w1, f1)], f1, c1, w1, big1)
        r1 = residual_of(v1, f1, c1, big1)
        own = []
        for d in range(2):
            G[d, 0:24, :] = r1[2 * d] + r1[2 * d + 1]
            pairs = G[d, pl.ds(8, 8, stride=2), :] + G[d, pl.ds(9, 8, stride=2), :]
            own.append(along_pairs(pairs, spot) * 0.125)
        AS[1 + cycle] = stack_depth(*own)
        peers, arrived = (NEARER, BL) if final else (AROUND, BF)
        to_far = start(far_copies(1 + cycle, arrived, peers), (arrived, FAR + 1 + cycle))
        for d in range(4):
            V1[d] = v1[d]
            E2[cycle, d] = two_in_one(F1[d, 8:16, :], V1[d, 8:16, :])
        to_mid = start(mid_copies(MID + 1 + cycle, E2.at[cycle], R2.at[cycle]), (R2.at[cycle], MID + 1 + cycle))

        if cycle == 0:
            arrive(to_more)
            unpack_edges(0, C, (0, 1, 8, 9), 1, 5)
            unpack_edges(0, C, (8, 9), 35, 39)
            unpack_edges(1, source, (0, 1), 2, 6)
            unpack_edges(1, source, (8, 9), 34, 38)
            mask_conductivity([*range(1, 5), *range(35, 39)])
            blur_rows(rows_of(C), 2, 6, coefficients, flux=False)
            blur_rows(rows_of(C), 34, 38, coefficients, flux=False)
            fine_sweep(source, scaled, 3, 7, put(VB))
            fine_sweep(source, scaled, 33, 37, put(VB))

            arrive(to_far_c)
            side = jnp.where(lane < 32, yes_left, jnp.where(lane < 64, 1.0, yes_right))
            spread_far(0, BC, AROUND, (C2, D2), side)
            c2 = load(C2, 2)
            diag = load(D2, 2)
            for d, w in enumerate(weight(c2, diag)):
                W2[d] = w
                D2[d] = diag[d] + 16.0 * c2[d]
            G3[...] = c2[0] + c2[1]
            pairs = G3[pl.ds(0, 24, stride=2), :] + G3[pl.ds(1, 24, stride=2), :]
            c3 = [along_pairs(pairs, twice) * (0.125 * 0.5)]
            diag = diagonal(c3, 3, 4.0)
            w3 = weight(c3, diag)
            big3 = [diag[0] + 8.0 * c3[0]]
            for j, v in enumerate((c3, w3, big3)):
                Z[j] = v[0]

        arrive(to_mid)

        def keep_1(g, d, a, b):
            F1[d, 8 * g : 8 * g + 8, :] = a
            V1[d, 8 * g : 8 * g + 8, :] = b * masks[g]

        mid_whole(E2.at[cycle], R2.at[cycle], keep_1)

        arrive(to_far)
        spread_far(1 + cycle, arrived, peers, (F2,), None)
        c2, w2, big2, f2 = load(C2, 2), load(W2, 2), load(D2, 2), load(F2, 2)
        v2 = sweep([w * f for w, f in zip(w2, f2)], f2, c2, w2, big2)
        for d in range(2):
            V2[d] = v2[d]
        r2 = residual_of(v2, f2, c2, big2)
        G3[...] = r2[0] + r2[1]

        pairs = G3[pl.ds(0, 24, stride=2), :] + G3[pl.ds(1, 24, stride=2), :]
        f3 = [along_pairs(pairs, twice) * 0.125]
        c3, w3, big3 = [Z[0]], [Z[1]], [Z[2]]
        v3 = [w3[0] * f3[0]]
        for _ in range(COARSE_SWEEPS - 1):
            v3 = sweep(v3, f3, c3, w3, big3)
        half = lane24 // 2
        up = pick(v3[0], half)
        H2[pl.ds(0, 24, stride=2), :] = up
        H2[pl.ds(1, 24, stride=2), :] = up

        c2, w2, big2, f2 = [[ref[d, 8:32, :] for d in range(2)] for ref in (C2, W2, D2, F2)]
        v2 = [V2[d, 8:32, :] + H2[8:32, :] for d in range(2)]
        for _ in range(2):
            v2 = sweep(v2, f2, c2, w2, big2)
        down = jnp.where(lane24 < 96, 32 + half, half - 32)
        for d in range(2):
            up = pick(v2[d], down)
            H1[d, pl.ds(0, 24, stride=2), :] = up
            H1[d, pl.ds(1, 24, stride=2), :] = up

        c1, w1, big1, f1 = load(C1, 4), load(W1, 4), load(D1, 4), load(F1, 4)
        v1 = [V1[d] + H1[d // 2, 16:40, :] for d in range(4)]
        for _ in range(2):
            v1 = sweep(v1, f1, c1, w1, big1)
        for d in range(8):
            T[0, pl.ds(d, 24, stride=8), :] = v1[d // 2]

        near = lane // 2
        for q in range((9 - wide) // 2 + 2, (30 + wide) // 2 + 3):
            row = T[0, 8 * q : 8 * q + 8, :]
            up = [pick(row, near), pick(row, 64 + near)]
            for r in (2 * q - 4, 2 * q - 3):
                for t in range(2):
                    VA[t, r] = VB[t, r] + up[t]
        fine_sweep(source, rows_of(VA), 10 - wide, 30 + wide, put(VB))

        def add(t, q, v):
            K[t, q] = v if cycle == 0 else K[t, q] + v

        fine_sweep(source, rows_of(VB), 11 - wide, 29 + wide, add)

        def keep_residual(q, spread, flux):
            if final:
                v = K[0, q]
                out[pl.ds(q - OWN, DEPTH, stride=WIDE), :] = v
                res[pl.ds(q - OWN, DEPTH, stride=WIDE), :] = fine_change(q, 0, v, F.at[0], spread, flux)
            else:
                for t in range(2):
                    F[cycle + 1, t, q] = fine_change(q, t, K[t, q], F.at[0], spread, flux)

        blur_rows(rows_of(K), 12 - wide, 28 + wide, keep_residual)

    for c in ends:
        c.wait_send()


def per_device(gx_count, gy_count, rhs, cond_class, charge_class, cond_table, charge_table):
    flat = (DEPTH * WIDE, LONG)
    f32, i32 = jnp.float32, jnp.int32
    tile = (8, 128)
    fine = pltpu.VMEM((2, 40) + tile, f32)
    mid = pltpu.VMEM((4, 24, 128), f32)
    low = pltpu.VMEM((2, 48, 128), f32)
    scratch = [
        pltpu.VMEM(flat, f32), pltpu.VMEM(flat, i32), pltpu.VMEM(flat, i32), pltpu.SMEM((16,), f32), pltpu.SMEM((16,), f32),
        fine, fine, fine, pltpu.VMEM((CYCLES, 2, 40) + tile, f32), fine, fine, fine,
        pltpu.VMEM((2, 4) + tile, f32), pltpu.VMEM((2, 2, 10) + tile, f32), pltpu.VMEM((2, 192, 128), f32),
        mid, mid, mid, mid, mid,
        pltpu.VMEM((2,) + tile, f32), pltpu.VMEM((8, 2) + tile, f32),
        pltpu.VMEM((CYCLES, 4) + tile, f32), pltpu.VMEM((CYCLES, 8, 4) + tile, f32),
        pltpu.VMEM((2, 32, 128), f32), pltpu.VMEM((2, 16, 128), f32),
        pltpu.VMEM((1 + CYCLES,) + tile, f32), pltpu.VMEM((len(AROUND),) + tile, f32),
        pltpu.VMEM((len(AROUND),) + tile, f32), pltpu.VMEM((len(NEARER),) + tile, f32),
        low, low, low, low, low, pltpu.VMEM((48, 128), f32),
        pltpu.VMEM((48, 128), f32), pltpu.VMEM((2, 48, 128), f32), pltpu.VMEM((3, 24, 128), f32),
        pltpu.SemaphoreType.DMA((COPIES,)), pltpu.SemaphoreType.DMA((COPIES,)), pltpu.SemaphoreType.DMA((5,)),
    ]
    hbm, vmem = pl.BlockSpec(memory_space=pl.ANY), pl.BlockSpec(memory_space=pltpu.VMEM)
    correction, residual = pl.pallas_call(
        functools.partial(kernel, gx_count, gy_count),
        out_shape=[pltpu.VMEM(flat, f32)] * 2,
        in_specs=[hbm] * 5,
        out_specs=[vmem, vmem],
        scratch_shapes=scratch,
        compiler_params=pltpu.CompilerParams(collective_id=0, has_side_effects=True),
    )(rhs.reshape(flat), cond_class.reshape(flat), charge_class.reshape(flat), cond_table, charge_table)
    return correction.reshape(rhs.shape), residual.reshape(rhs.shape)


def solution(mesh):
    placed = (P(None, "gx", "gy"), P(None, "gx", "gy"), P(None, "gx", "gy"), P(), P())
    return jax.shard_map(
        functools.partial(per_device, mesh.shape["gx"], mesh.shape["gy"]),
        mesh=mesh,
        in_specs=placed,
        out_specs=(P(None, "gx", "gy"), P(None, "gx", "gy")),
        check_vma=False,
    )
```

time: 52 us -> 48.1 us (0.925)
  the two profiles are of different devices: /device:TPU:2 before, /device:TPU:1 now
where the time goes in v2:
time: 48.1 us; the launch traced here: 48 us
  Pallas kernels  46.1 us (96%)
  local copies, waits for them, and re-layouts  1.26 us (3%)
  between operations  0.64 us (1%)
    pallas_call x1, Pallas kernels, per_device(): pl.pallas_call(functools.partial(kernel, gx_count, gy_count), out_shape=[...  46.1 us
    unnamed x2, local copies, waits for them, and re-layouts  1.26 us

profile of v2, /device:TPU:1, one launch (start us, length us, event | category | flops | bytes accessed | tf_op | source)
XLA Modules:
  0.0 48.0 jit_solution(4636227143845550216)
XLA Ops:
  0.6 46.1 %shard_map.68 = (f32[128,128]{1,0:T(8,128)S(1)}, f32[128,128]{1,0:T(8,128)S(1)}) custom-call(f32[128,128]{1,0:T(8,128)} %bitcast.7, s32[128,128]{1,0:T(8,128)} %bitcast.8, s32[128,128]{1,0:T(8,128)} %bitcast.9, f32[16]{0:T(128)} %cond_table_in.1, f32[16]{0:T(128)} %charge_table_in.1), custom_call_target="tpu_custom_call" | custom-call | tf_op jit(solution)/shard_map/pallas_call | solution.py:522
  46.7 0.6 %copy.9 = f32[8,16,128]{2,1,0:T(8,128)} copy(f32[8,16,128]{2,1,0:T(8,128)S(1)} %bitcast.6) | data formatting | bytes 131072
  47.3 0.6 %copy.10 = f32[8,16,128]{2,1,0:T(8,128)} copy(f32[8,16,128]{2,1,0:T(8,128)S(1)} %bitcast.5) | data formatting | bytes 131072

commit v3 on v2

--- a/solution.py
+++ b/solution.py
@@ -149,12 +149,9 @@
                     array[1, 4 * b + i] = roll(packed, -(32 * i + 16), 1)
 
     def blur_row(t0, t1):
-        b0, b1 = roll(t0, -1, 1), roll(t1, -1, 1)
-        u0 = t0 + jnp.where(last, b1, b0)
-        u1 = t1 + jnp.where(last, b0, b1)
-        a0, a1 = roll(u0, 1, 1), roll(u1, 1, 1)
-        y0 = u0 + jnp.where(first, a1, a0)
-        y1 = u1 + jnp.where(first, a0, a1)
+        a0, a1, b0, b1 = roll(t0, 1, 1), roll(t1, 1, 1), roll(t0, -1, 1), roll(t1, -1, 1)
+        y0 = (t0 + t0) + (jnp.where(first, a1, a0) + jnp.where(last, b1, b0))
+        y1 = (t1 + t1) + (jnp.where(first, a0, a1) + jnp.where(last, b0, b1))
         return [y + (above * roll(y, 1, 0) + below * roll(y, -1, 0)) for y in (y0, y1)]
 
     def blur_rows(row, lo, hi, use, flux=True):

time: 48.1 us -> 44.1 us (0.917)
  Pallas kernels: 46.1 us -> 42 us
    pallas_call x1, Pallas kernels: 46.1 us -> 42 us  [per_device(): pl.pallas_call(functools.partial(kernel, gx_count, gy_count), out_shape=[...]
where the time goes in v3:
time: 44.1 us; the launch traced here: 43.9 us
  Pallas kernels  42 us (95%)
  local copies, waits for them, and re-layouts  1.26 us (3%)
  between operations  0.64 us (1%)
    pallas_call x1, Pallas kernels, per_device(): pl.pallas_call(functools.partial(kernel, gx_count, gy_count), out_shape=[...  42 us
    unnamed x2, local copies, waits for them, and re-layouts  1.26 us

profile of v3, /device:TPU:1, one launch (start us, length us, event | category | flops | bytes accessed | tf_op | source)
XLA Modules:
  0.0 43.9 jit_solution(5640791587243377759)
XLA Ops:
  0.6 42.0 %shard_map.68 = (f32[128,128]{1,0:T(8,128)S(1)}, f32[128,128]{1,0:T(8,128)S(1)}) custom-call(f32[128,128]{1,0:T(8,128)} %bitcast.7, s32[128,128]{1,0:T(8,128)} %bitcast.8, s32[128,128]{1,0:T(8,128)} %bitcast.9, f32[16]{0:T(128)} %cond_table_in.1, f32[16]{0:T(128)} %charge_table_in.1), custom_call_target="tpu_custom_call" | custom-call | tf_op jit(solution)/shard_map/pallas_call | solution.py:519
  42.7 0.6 %copy.9 = f32[8,16,128]{2,1,0:T(8,128)} copy(f32[8,16,128]{2,1,0:T(8,128)S(1)} %bitcast.6) | data formatting | bytes 131072
  43.3 0.6 %copy.10 = f32[8,16,128]{2,1,0:T(8,128)} copy(f32[8,16,128]{2,1,0:T(8,128)S(1)} %bitcast.5) | data formatting | bytes 131072

commit v4 on v3

--- a/solution.py
+++ b/solution.py
@@ -15,11 +15,11 @@
 DEPTH, WIDE, LONG = 8, 16, 128
 OWN = 12
 SIDES = ((1, 0), (-1, 0), (0, 1), (0, -1), (1, 1), (1, -1), (-1, 1), (-1, -1))
-AROUND = tuple((a, b) for a in range(-5, 6) for b in (-1, 0, 1) if (a, b) != (0, 0))
+AROUND = tuple((s * a, b) for b in (-1, 1, 0) for a in (5, 2, 3, 1, 4, 0) for s in ((1, -1) if a else (1,)) if a or b)
 NEARER = tuple(p for p in AROUND if abs(p[0]) < 5)
 
 FINE, FINE_MORE, MID, FAR = 0, 16, 28, 31
-COPIES = 34
+COPIES = 33
 
 
 def roll(x, shift, axis):
@@ -75,7 +75,7 @@
 
 def kernel(gx_count, gy_count, rhs_in, cond_in, charge_in, cond_table_in, charge_table_in, out, res, *scratch):
     (rhs, cond, charge, cond_table, charge_table, C, W, D, F, VA, VB, K, PS, PR, T, C1, W1, D1, F1, V1, E1, R1, E2, R2, G, S2,
-     AS, BC, BF, BL, C2, W2, D2, F2, V2, G3, H2, H1, Z, send_sem, recv_sem, in_sem) = scratch
+     AS, AL, BF, BL, C2, W2, D2, F2, V2, G3, H2, H1, Z, send_sem, recv_sem, in_sem) = scratch
     gx, gy = lax.axis_index("gx"), lax.axis_index("gy")
 
     def at(dx, dy):
@@ -87,13 +87,13 @@
             device_id=where, device_id_type=MESH,
         )
 
-    barrier = pltpu.get_barrier_semaphore()
-    for peer in AROUND:
-        pl.semaphore_signal(barrier, inc=1, device_id=at(*peer), device_id_type=MESH)
     pairs = ((cond_table_in, cond_table), (charge_table_in, charge_table), (cond_in, cond), (charge_in, charge), (rhs_in, rhs))
     inputs = [pltpu.make_async_copy(a, b, in_sem.at[i]) for i, (a, b) in enumerate(pairs)]
     for c in inputs:
         c.start()
+    barrier = pltpu.get_barrier_semaphore()
+    for peer in AROUND:
+        pl.semaphore_signal(barrier, inc=1, device_id=at(*peer), device_id_type=MESH)
 
     left_in, right_in = gy > 0, gy < gy_count - 1
     low_in = jnp.where(gx > 0, 1.0, 0.0)
@@ -119,7 +119,7 @@
             (PS.at[n, pl.ds(0, 2)], PR.at[n, 0, pl.ds(7, 2)]),
             (PS.at[n, pl.ds(0, 2)], PR.at[n, 1, pl.ds(7, 2)]),
         )
-        return [copy(a, b, FINE + 8 * n + i, at(*SIDES[i])) for i, (a, b) in enumerate(ends)]
+        return [copy(*ends[i], FINE + 8 * n + i, at(*SIDES[i])) for i in (4, 5, 6, 7, 0, 1, 2, 3)]
 
     def more_copies(n, array, h):
         ends = (
@@ -236,29 +236,35 @@
     mid_side = jnp.where(lane < 64, 1.0, jnp.where(lane < 96, yes_right, yes_left))
     masks = (mid_side * low_in, mid_side, mid_side * high_in)
 
-    def far_copies(n, target, peers):
-        return [copy(AS.at[n], target.at[i], FAR + n, at(*p)) for i, p in enumerate(peers)]
-
-    def far_block(n, arrived, peers, a, split):
+    def far_copies(n, source, target, peers):
+        return [copy(source, target.at[i], FAR + n, at(*p)) for i, p in enumerate(peers)]
+
+    def by_side(left, middle, right):
+        return jnp.where(lane < 32, left, jnp.where(lane < 64, middle, right))
+
+    def first_block(a):
+        parts = [AS[0] if (a, b) == (0, 0) else BF[AROUND.index((-a, -b))] for b in (-1, 0, 1)]
+        return [by_side(*[roll(v, 32 * (k - j), 1) for k, v in enumerate(parts)]) for j in range(3)]
+
+    unfold = 32 * lax.rem(sub, 4) + lax.rem(lane, 32)
+
+    def later_block(a):
         parts = []
         for b in (-1, 0, 1):
-            parts.append(AS[n] if (a, b) == (0, 0) else arrived[peers.index((-a, -b))])
-        if not split:
-            return [jnp.where(lane < 32, parts[0], jnp.where(lane < 64, parts[1], parts[2]))]
-        turned = [roll(p, 32, 1) for p in parts]
-        return [
-            jnp.where(lane < 32, parts[0], jnp.where(lane < 64, turned[1], parts[2])),
-            jnp.where(lane < 32, turned[0], jnp.where(lane < 64, parts[1], turned[2])),
-        ]
-
-    def spread_far(n, arrived, peers, arrays, mask):
-        split = len(arrays) == 2
+            if (a, b) == (0, 0):
+                parts.append(AS[1])
+            else:
+                k = NEARER.index((-a, -b))
+                rows = [jnp.broadcast_to(BL[k, d : d + 1, :], (8, 128)) for d in range(2)]
+                parts.append(pick(jnp.where(sub < 4, *rows), unfold))
+        return [by_side(*parts)]
+
+    def spread_far(block, reach, arrays, mask):
         zero = jnp.zeros((8, 128), jnp.float32)
-        reach = max(p[0] for p in peers)
         for g in range(6):
             pair = []
             for a in (2 * g - 5, 2 * g - 4):
-                blocks = far_block(n, arrived, peers, a, split) if abs(a) <= reach else [zero] * len(arrays)
+                blocks = block(a) if abs(a) <= reach else [zero] * len(arrays)
                 if mask is not None and abs(a) <= reach:
                     there = jnp.where(jnp.logical_and(gx + a >= 0, gx + a < gx_count), 1.0, 0.0)
                     blocks[0] = blocks[0] * (mask * there)
@@ -361,18 +367,16 @@
             for d in range(2):
                 G[d, 0:24, :] = c1[2 * d] + c1[2 * d + 1]
             c2 = []
-            own = []
+            own_c = []
             for d in range(2):
                 pairs = G[d, pl.ds(0, 16, stride=2), :] + G[d, pl.ds(1, 16, stride=2), :]
                 c2.append(along_pairs(pairs, twice[:16]) * (0.125 * 0.25))
                 pairs = G[d, pl.ds(8, 8, stride=2), :] + G[d, pl.ds(9, 8, stride=2), :]
-                own.append(along_pairs(pairs, spot) * (0.125 * 0.25))
+                own_c.append(along_pairs(pairs, spot) * (0.125 * 0.25))
             own_d = []
             for d, v in enumerate(diagonal(c2, 2, 8.0)):
                 S2[d] = v
                 own_d.append(pick(S2[d, 4:12, :], spot // 2))
-            AS[0] = jnp.where(lax.rem(lane, 64) < 32, stack_depth(*own), stack_depth(*own_d))
-            to_far_c = start(far_copies(0, BC, AROUND), (BC, FAR))
 
         c1, w1, big1 = load(C1, 4), load(W1, 4), load(D1, 4)
         f1 = load(F1, 4)
@@ -383,9 +387,17 @@
             G[d, 0:24, :] = r1[2 * d] + r1[2 * d + 1]
             pairs = G[d, pl.ds(8, 8, stride=2), :] + G[d, pl.ds(9, 8, stride=2), :]
             own.append(along_pairs(pairs, spot) * 0.125)
-        AS[1 + cycle] = stack_depth(*own)
-        peers, arrived = (NEARER, BL) if final else (AROUND, BF)
-        to_far = start(far_copies(1 + cycle, arrived, peers), (arrived, FAR + 1 + cycle))
+        own = stack_depth(*own)
+        if cycle == 0:
+            AS[0] = jnp.where(lane < 32, stack_depth(*own_c), jnp.where(lane < 64, stack_depth(*own_d), own))
+            to_far = start(far_copies(0, AS.at[0], BF, AROUND), (BF, FAR))
+        else:
+            AS[1] = own
+            one = jnp.where(lane // 32 == lax.rem(sub, 4), own, 0.0)
+            one = one + roll(one, -1, 0)
+            one = one + roll(one, -2, 0)
+            AL[...] = jnp.where(sub == 0, one, roll(one, -3, 0))[0:2]
+            to_far = start(far_copies(1, AL, BL, NEARER), (BL, FAR + 1))
         for d in range(4):
             V1[d] = v1[d]
             E2[cycle, d] = two_in_one(F1[d, 8:16, :], V1[d, 8:16, :])
@@ -403,14 +415,23 @@
             fine_sweep(source, scaled, 3, 7, put(VB))
             fine_sweep(source, scaled, 33, 37, put(VB))
 
-            arrive(to_far_c)
+        arrive(to_far)
+        if cycle == 0:
             side = jnp.where(lane < 32, yes_left, jnp.where(lane < 64, 1.0, yes_right))
-            spread_far(0, BC, AROUND, (C2, D2), side)
+            spread_far(first_block, 5, (C2, D2, F2), side)
             c2 = load(C2, 2)
             diag = load(D2, 2)
             for d, w in enumerate(weight(c2, diag)):
                 W2[d] = w
                 D2[d] = diag[d] + 16.0 * c2[d]
+        else:
+            spread_far(later_block, 4, (F2,), None)
+        c2, w2, big2, f2 = load(C2, 2), load(W2, 2), load(D2, 2), load(F2, 2)
+        v2 = sweep([w * f for w, f in zip(w2, f2)], f2, c2, w2, big2)
+        for d in range(2):
+            V2[d] = v2[d]
+        r2 = residual_of(v2, f2, c2, big2)
+        if cycle == 0:
             G3[...] = c2[0] + c2[1]
             pairs = G3[pl.ds(0, 24, stride=2), :] + G3[pl.ds(1, 24, stride=2), :]
             c3 = [along_pairs(pairs, twice) * (0.125 * 0.5)]
@@ -419,25 +440,9 @@
             big3 = [diag[0] + 8.0 * c3[0]]
             for j, v in enumerate((c3, w3, big3)):
                 Z[j] = v[0]
-
-        arrive(to_mid)
-
-        def keep_1(g, d, a, b):
-            F1[d, 8 * g : 8 * g + 8, :] = a
-            V1[d, 8 * g : 8 * g + 8, :] = b * masks[g]
-
-        mid_whole(E2.at[cycle], R2.at[cycle], keep_1)
-
-        arrive(to_far)
-        spread_far(1 + cycle, arrived, peers, (F2,), None)
-        c2, w2, big2, f2 = load(C2, 2), load(W2, 2), load(D2, 2), load(F2, 2)
-        v2 = sweep([w * f for w, f in zip(w2, f2)], f2, c2, w2, big2)
-        for d in range(2):
-            V2[d] = v2[d]
-        r2 = residual_of(v2, f2, c2, big2)
-        G3[...] = r2[0] + r2[1]
-
-        pairs = G3[pl.ds(0, 24, stride=2), :] + G3[pl.ds(1, 24, stride=2), :]
+        H2[...] = r2[0] + r2[1]
+
+        pairs = H2[pl.ds(0, 24, stride=2), :] + H2[pl.ds(1, 24, stride=2), :]
         f3 = [along_pairs(pairs, twice) * 0.125]
         c3, w3, big3 = [Z[0]], [Z[1]], [Z[2]]
         v3 = [w3[0] * f3[0]]
@@ -458,6 +463,13 @@
             H1[d, pl.ds(0, 24, stride=2), :] = up
             H1[d, pl.ds(1, 24, stride=2), :] = up
 
+        arrive(to_mid)
+
+        def keep_1(g, d, a, b):
+            F1[d, 8 * g : 8 * g + 8, :] = a
+            V1[d, 8 * g : 8 * g + 8, :] = b * masks[g]
+
+        mid_whole(E2.at[cycle], R2.at[cycle], keep_1)
         c1, w1, big1, f1 = load(C1, 4), load(W1, 4), load(D1, 4), load(F1, 4)
         v1 = [V1[d] + H1[d // 2, 16:40, :] for d in range(4)]
         for _ in range(2):
@@ -509,8 +521,8 @@
         pltpu.VMEM((2,) + tile, f32), pltpu.VMEM((8, 2) + tile, f32),
         pltpu.VMEM((CYCLES, 4) + tile, f32), pltpu.VMEM((CYCLES, 8, 4) + tile, f32),
         pltpu.VMEM((2, 32, 128), f32), pltpu.VMEM((2, 16, 128), f32),
-        pltpu.VMEM((1 + CYCLES,) + tile, f32), pltpu.VMEM((len(AROUND),) + tile, f32),
-        pltpu.VMEM((len(AROUND),) + tile, f32), pltpu.VMEM((len(NEARER),) + tile, f32),
+        pltpu.VMEM((2,) + tile, f32), pltpu.VMEM((2, 128), f32),
+        pltpu.VMEM((len(AROUND),) + tile, f32), pltpu.VMEM((len(NEARER), 2, 128), f32),
         low, low, low, low, low, pltpu.VMEM((48, 128), f32),
         pltpu.VMEM((48, 128), f32), pltpu.VMEM((2, 48, 128), f32), pltpu.VMEM((3, 24, 128), f32),
         pltpu.SemaphoreType.DMA((COPIES,)), pltpu.SemaphoreType.DMA((COPIES,)), pltpu.SemaphoreType.DMA((5,)),

time: 44.1 us -> 40.6 us (0.921)
  Pallas kernels: 42 us -> 38.5 us
    pallas_call x1, Pallas kernels: 42 us -> 38.5 us  [per_device(): pl.pallas_call(functools.partial(kernel, gx_count, gy_count), out_shape=[...]
where the time goes in v4:
time: 40.6 us; the launch traced here: 40.4 us
  Pallas kernels  38.5 us (95%)
  local copies, waits for them, and re-layouts  1.26 us (3%)
  between operations  0.64 us (2%)
    pallas_call x1, Pallas kernels, per_device(): pl.pallas_call(functools.partial(kernel, gx_count, gy_count), out_shape=[...  38.5 us
    unnamed x2, local copies, waits for them, and re-layouts  1.26 us

profile of v4, /device:TPU:1, one launch (start us, length us, event | category | flops | bytes accessed | tf_op | source)
XLA Modules:
  0.0 40.4 jit_solution(14220123606942671889)
XLA Ops:
  0.6 38.5 %shard_map.68 = (f32[128,128]{1,0:T(8,128)S(1)}, f32[128,128]{1,0:T(8,128)S(1)}) custom-call(f32[128,128]{1,0:T(8,128)} %bitcast.7, s32[128,128]{1,0:T(8,128)} %bitcast.8, s32[128,128]{1,0:T(8,128)} %bitcast.9, f32[16]{0:T(128)} %cond_table_in.1, f32[16]{0:T(128)} %charge_table_in.1), custom_call_target="tpu_custom_call" | custom-call | tf_op jit(solution)/shard_map/pallas_call | solution.py:531
  39.1 0.6 %copy.9 = f32[8,16,128]{2,1,0:T(8,128)} copy(f32[8,16,128]{2,1,0:T(8,128)S(1)} %bitcast.6) | data formatting | bytes 131072
  39.8 0.6 %copy.10 = f32[8,16,128]{2,1,0:T(8,128)} copy(f32[8,16,128]{2,1,0:T(8,128)S(1)} %bitcast.5) | data formatting | bytes 131072

commit v5 on v4

--- a/solution.py
+++ b/solution.py
@@ -18,8 +18,8 @@
 AROUND = tuple((s * a, b) for b in (-1, 1, 0) for a in (5, 2, 3, 1, 4, 0) for s in ((1, -1) if a else (1,)) if a or b)
 NEARER = tuple(p for p in AROUND if abs(p[0]) < 5)
 
-FINE, FINE_MORE, MID, FAR = 0, 16, 28, 31
-COPIES = 33
+FINE, FINE_MORE, MID, FAR = 0, 2, 4, 7
+COPIES = 9
 
 
 def roll(x, shift, axis):
@@ -119,7 +119,7 @@
             (PS.at[n, pl.ds(0, 2)], PR.at[n, 0, pl.ds(7, 2)]),
             (PS.at[n, pl.ds(0, 2)], PR.at[n, 1, pl.ds(7, 2)]),
         )
-        return [copy(*ends[i], FINE + 8 * n + i, at(*SIDES[i])) for i in (4, 5, 6, 7, 0, 1, 2, 3)]
+        return [copy(*ends[i], FINE + n, at(*SIDES[i])) for i in (4, 5, 6, 7, 0, 1, 2, 3)]
 
     def more_copies(n, array, h):
         ends = (
@@ -130,7 +130,7 @@
             (PS.at[n, 2], PR.at[n, 0, 9], 6),
             (PS.at[n, 2], PR.at[n, 1, 9], 7),
         )
-        return [copy(a, b, FINE_MORE + 6 * n + i, at(*SIDES[k])) for i, (a, b, k) in enumerate(ends)]
+        return [copy(a, b, FINE_MORE + n, at(*SIDES[k])) for i, (a, b, k) in enumerate(ends)]
 
     def pack_edges(n, array):
         for b in range(4):
@@ -218,7 +218,7 @@
         return jnp.where(lane < 64, a, roll(b, 64, 1))
 
     def mid_copies(number, source, target):
-        return [copy(source, target.at[i], number, at(*SIDES[i])) for i in range(8)]
+        return [copy(source, target.at[i], number, at(*SIDES[i])) for i in (4, 5, 6, 7, 0, 1, 2, 3)]
 
     def mid_whole(own, arrived, keep):
         for g, (middle, before, after) in enumerate(((0, 4, 5), (None, 2, 3), (1, 6, 7))):
@@ -312,10 +312,11 @@
         E1[d] = two_in_one(own[d], own[d + 2])
 
     pl.semaphore_wait(barrier, len(AROUND))
-    to_c = start(fine_copies(0, C, 7))
-    to_f = start(fine_copies(1, F.at[0], 6))
+    to_c = start(fine_copies(0, C, 7), (C.at[0, pl.ds(0, 30)], FINE))
+    to_f = start(fine_copies(1, F.at[0], 6), (F.at[0, 0, pl.ds(0, 28)], FINE + 1))
     to_c1 = start(mid_copies(MID, E1, R1), (R1, MID))
-    to_more = start(more_copies(0, C, 7)) + start(more_copies(1, F.at[0], 6))
+    to_more = start(more_copies(0, C, 7), (C.at[0, pl.ds(0, 12)], FINE_MORE))
+    to_more += start(more_copies(1, F.at[0], 6), (F.at[0, 0, pl.ds(0, 12)], FINE_MORE + 1))
 
     arrive(to_c)
     unpack_edges(0, C, range(1, 9), 5, 35)
@@ -398,10 +399,14 @@
             one = one + roll(one, -2, 0)
             AL[...] = jnp.where(sub == 0, one, roll(one, -3, 0))[0:2]
             to_far = start(far_copies(1, AL, BL, NEARER), (BL, FAR + 1))
+
+        def send_mid():
+            return start(mid_copies(MID + 1 + cycle, E2.at[cycle], R2.at[cycle]), (R2.at[cycle], MID + 1 + cycle))
+
         for d in range(4):
             V1[d] = v1[d]
             E2[cycle, d] = two_in_one(F1[d, 8:16, :], V1[d, 8:16, :])
-        to_mid = start(mid_copies(MID + 1 + cycle, E2.at[cycle], R2.at[cycle]), (R2.at[cycle], MID + 1 + cycle))
+        to_mid = send_mid()
 
         if cycle == 0:
             arrive(to_more)

time: 40.6 us -> 40.1 us (0.988)
  Pallas kernels: 38.5 us -> 38 us
    pallas_call x1, Pallas kernels: 38.5 us -> 38 us  [per_device(): pl.pallas_call(functools.partial(kernel, gx_count, gy_count), out_shape=[...]
where the time goes in v5:
time: 40.1 us; the launch traced here: 39.9 us
  Pallas kernels  38 us (95%)
  local copies, waits for them, and re-layouts  1.26 us (3%)
  between operations  0.64 us (2%)
    pallas_call x1, Pallas kernels, per_device(): pl.pallas_call(functools.partial(kernel, gx_count, gy_count), out_shape=[...  38 us
    unnamed x2, local copies, waits for them, and re-layouts  1.26 us

profile of v5, /device:TPU:1, one launch (start us, length us, event | category | flops | bytes accessed | tf_op | source)
XLA Modules:
  0.0 39.9 jit_solution(5277843734814880024)
XLA Ops:
  0.6 38.0 %shard_map.68 = (f32[128,128]{1,0:T(8,128)S(1)}, f32[128,128]{1,0:T(8,128)S(1)}) custom-call(f32[128,128]{1,0:T(8,128)} %bitcast.7, s32[128,128]{1,0:T(8,128)} %bitcast.8, s32[128,128]{1,0:T(8,128)} %bitcast.9, f32[16]{0:T(128)} %cond_table_in.1, f32[16]{0:T(128)} %charge_table_in.1), custom_call_target="tpu_custom_call" | custom-call | tf_op jit(solution)/shard_map/pallas_call | solution.py:536
  38.7 0.6 %copy.9 = f32[8,16,128]{2,1,0:T(8,128)} copy(f32[8,16,128]{2,1,0:T(8,128)S(1)} %bitcast.6) | data formatting | bytes 131072
  39.3 0.6 %copy.10 = f32[8,16,128]{2,1,0:T(8,128)} copy(f32[8,16,128]{2,1,0:T(8,128)S(1)} %bitcast.5) | data formatting | bytes 131072

commit v6 on v5

--- a/solution.py
+++ b/solution.py
@@ -155,7 +155,7 @@
         return [y + (above * roll(y, 1, 0) + below * roll(y, -1, 0)) for y in (y0, y1)]
 
     def blur_rows(row, lo, hi, use, flux=True):
-        before = pair = None
+        before = pair = held_v = None
         for r in range(lo - 1, hi + 1):
             v = row(r)
             fields = [v, [C[t, r] * v[t] for t in range(2)]] if flux else [v]
@@ -163,16 +163,15 @@
             if before is not None:
                 two = [[a + b for a, b in zip(x, y)] for x, y in zip(before, now)]
                 if pair is not None:
-                    use(r - 1, *[[a + b for a, b in zip(x, y)] for x, y in zip(pair, two)])
+                    use(r - 1, held_v, *[[a + b for a, b in zip(x, y)] for x, y in zip(pair, two)])
                 pair = two
-            before = now
+            before, held_v = now, v
 
     def fine_change(q, t, v, f, spread, flux):
         return f[t, q] - (D[t, q] * v - (C[t, q] * spread[t] + flux[t]))
 
     def fine_sweep(source, row, lo, hi, keep):
-        def use(q, spread, flux):
-            v = row(q)
+        def use(q, v, spread, flux):
             for t in range(2):
                 keep(t, q, v[t] + W[t, q] * fine_change(q, t, v[t], source, spread, flux))
 
@@ -197,9 +196,9 @@
                 C[0, r] = C[0, r] * mask
                 C[1, r] = C[1, r] * (side * mask)
 
-    def coefficients(q, spread):
+    def coefficients(q, v, spread):
         for t in range(2):
-            c = C[t, q]
+            c = v[t]
             diag = (4.0 * (6.0 + SHIFT)) * c + spread[t]
             inside = c > 0.0
             D[t, q] = diag + 8.0 * c
@@ -338,8 +337,7 @@
         fine_sweep(source, scaled, 7, 33, put(VB))
         held = {}
 
-        def pair_up(q, spread, flux):
-            v = [VB[0, q], VB[1, q]]
+        def pair_up(q, v, spread, flux):
             for t in range(2):
                 change = fine_change(q, t, v[t], source, spread, flux)
                 if q % 2 == 0:
@@ -496,14 +494,13 @@
 
         fine_sweep(source, rows_of(VB), 11 - wide, 29 + wide, add)
 
-        def keep_residual(q, spread, flux):
+        def keep_residual(q, v, spread, flux):
             if final:
-                v = K[0, q]
-                out[pl.ds(q - OWN, DEPTH, stride=WIDE), :] = v
-                res[pl.ds(q - OWN, DEPTH, stride=WIDE), :] = fine_change(q, 0, v, F.at[0], spread, flux)
+                out[pl.ds(q - OWN, DEPTH, stride=WIDE), :] = v[0]
+                res[pl.ds(q - OWN, DEPTH, stride=WIDE), :] = fine_change(q, 0, v[0], F.at[0], spread, flux)
             else:
                 for t in range(2):
-                    F[cycle + 1, t, q] = fine_change(q, t, K[t, q], F.at[0], spread, flux)
+                    F[cycle + 1, t, q] = fine_change(q, t, v[t], F.at[0], spread, flux)
 
         blur_rows(rows_of(K), 12 - wide, 28 + wide, keep_residual)
 

time: 40.1 us -> 40.1 us (level)
  no operation moved by 1% of the time
where the time goes in v6:
time: 40.1 us; the launch traced here: 39.9 us
  Pallas kernels  38 us (95%)
  local copies, waits for them, and re-layouts  1.26 us (3%)
  between operations  0.64 us (2%)
    pallas_call x1, Pallas kernels, per_device(): pl.pallas_call(functools.partial(kernel, gx_count, gy_count), out_shape=[...  38 us
    unnamed x2, local copies, waits for them, and re-layouts  1.26 us

profile of v6, /device:TPU:1, one launch (start us, length us, event | category | flops | bytes accessed | tf_op | source)
XLA Modules:
  0.0 39.9 jit_solution(524070463651157223)
XLA Ops:
  0.6 38.0 %shard_map.68 = (f32[128,128]{1,0:T(8,128)S(1)}, f32[128,128]{1,0:T(8,128)S(1)}) custom-call(f32[128,128]{1,0:T(8,128)} %bitcast.7, s32[128,128]{1,0:T(8,128)} %bitcast.8, s32[128,128]{1,0:T(8,128)} %bitcast.9, f32[16]{0:T(128)} %cond_table_in.1, f32[16]{0:T(128)} %charge_table_in.1), custom_call_target="tpu_custom_call" | custom-call | tf_op jit(solution)/shard_map/pallas_call | solution.py:533
  38.7 0.6 %copy.9 = f32[8,16,128]{2,1,0:T(8,128)} copy(f32[8,16,128]{2,1,0:T(8,128)S(1)} %bitcast.6) | data formatting | bytes 131072
  39.3 0.6 %copy.10 = f32[8,16,128]{2,1,0:T(8,128)} copy(f32[8,16,128]{2,1,0:T(8,128)S(1)} %bitcast.5) | data formatting | bytes 131072

commit v7 on v5

--- a/solution.py
+++ b/solution.py
@@ -92,7 +92,7 @@
     for c in inputs:
         c.start()
     barrier = pltpu.get_barrier_semaphore()
-    for peer in AROUND:
+    for peer in AROUND[::-1]:
         pl.semaphore_signal(barrier, inc=1, device_id=at(*peer), device_id_type=MESH)
 
     left_in, right_in = gy > 0, gy < gy_count - 1

time: 40.1 us -> 40.2 us (level)
  no operation moved by 1% of the time
where the time goes in v7:
time: 40.2 us; the launch traced here: 40.1 us
  Pallas kernels  38.2 us (95%)
  local copies, waits for them, and re-layouts  1.26 us (3%)
  between operations  0.64 us (2%)
    pallas_call x1, Pallas kernels, per_device(): pl.pallas_call(functools.partial(kernel, gx_count, gy_count), out_shape=[...  38.2 us
    unnamed x2, local copies, waits for them, and re-layouts  1.26 us

profile of v7, /device:TPU:1, one launch (start us, length us, event | category | flops | bytes accessed | tf_op | source)
XLA Modules:
  0.0 40.1 jit_solution(8126657115750466123)
XLA Ops:
  0.6 38.2 %shard_map.68 = (f32[128,128]{1,0:T(8,128)S(1)}, f32[128,128]{1,0:T(8,128)S(1)}) custom-call(f32[128,128]{1,0:T(8,128)} %bitcast.7, s32[128,128]{1,0:T(8,128)} %bitcast.8, s32[128,128]{1,0:T(8,128)} %bitcast.9, f32[16]{0:T(128)} %cond_table_in.1, f32[16]{0:T(128)} %charge_table_in.1), custom_call_target="tpu_custom_call" | custom-call | tf_op jit(solution)/shard_map/pallas_call | solution.py:536
  38.8 0.6 %copy.9 = f32[8,16,128]{2,1,0:T(8,128)} copy(f32[8,16,128]{2,1,0:T(8,128)S(1)} %bitcast.6) | data formatting | bytes 131072
  39.4 0.6 %copy.10 = f32[8,16,128]{2,1,0:T(8,128)} copy(f32[8,16,128]{2,1,0:T(8,128)S(1)} %bitcast.5) | data formatting | bytes 131072
